TPU v7x, 32 devices: a whole 2x2x4 slice. The times are simulated.
32 devices in a mesh: groups: 2 (over y), seq: 16 (over z, x, core).
Axes of the slice: x: 2, y: 2, z: 4, core: 2. Of those that a mesh axis runs over, the one named last changes fastest.
Arguments:
- queries: bfloat16 [8192, 2048], P(('groups', 'seq')), parts along dimension 0, may hold values from -128 to 128
- keys: bfloat16 [32768, 1024], P(('groups', 'seq')), parts along dimension 0, may hold values from -6 to 6
- values: bfloat16 [32768, 1024], P(('groups', 'seq')), parts along dimension 0, may hold values from -6 to 6
- dirty: int32 [32], P(('groups', 'seq')), parts along dimension 0, may hold values from -1 to 3
- spans: int32 [32, 2], P(('groups', 'seq')), parts along dimension 0, may hold values from 0 to 16384, as said below
Outputs:
- attended: bfloat16 [8192, 2048], P(('groups', 'seq')), parts along dimension 0
There are 2 independent parts, one for each index of `groups`. A program takes and returns all parts, laid end to end along the dimension named above; each array names one. Nothing has to cross between parts.
Inputs may be any that keep to these rules, and one draw needn't show every extreme that they name: -1 marks a shard with no dirty block. `spans`: row k holds the start and the exclusive end of the one tombstoned span of shard k: k * 1024 <= start < end <= (k + 1) * 1024, with end - start from 1 to 32; the last shard's span has exactly 32 rows.
All inputs are finite; a program needn't handle non-finite values.
Results may differ from a plain program's by a relative error of at most 0.014.
Values may be sent and summed in bfloat16 or wider, within the bound.
No kernel may reach another device: no remote copies, remote signals or barrier semaphores. Data moves between devices by JAX's collectives and lax.ppermute only.
A program may use at most 128 MiB of HBM per device.

v0:
```python
import math

import jax
import jax.numpy as jnp
from jax import lax
from jax.sharding import PartitionSpec as P

HEAD_DIMENSION = 128
WINDOW = 4096
BLOCK_ROWS = 256


softcap_limit = 50.0
query_scale = 144.0 ** (-0.5)


def from_behind(array, axis, by):
    count = lax.axis_size(axis)
    pairs = [(i, i + by) for i in range(count) if 0 <= i + by < count]
    return lax.ppermute(array, axis, pairs)


def locate(raw, spans):
    begin = spans[:, 0]
    finish = spans[:, 1]
    offset = raw[:, None] - begin[None, :]
    before = jnp.sum(jnp.clip(offset, 0, (finish - begin)[None, :]), axis=1)
    inside = jnp.sum(
        ((raw[:, None] >= begin[None, :]) & (raw[:, None] < finish[None, :])).astype(jnp.int32),
        axis=1,
    )
    return (raw - before, (inside == 0) & (raw >= 0))


def apply_rotary(field, place):
    half = field.shape[-1] // 2
    order = jnp.arange(half, dtype=jnp.float32)
    freq = jnp.exp(order * (-2.0 * math.log(10000.0) / field.shape[-1]))
    angle = place[:, None] * freq[None, :]
    cosine = jnp.cos(angle)[:, None, :]
    sine = jnp.sin(angle)[:, None, :]
    first = field[..., :half]
    second = field[..., half:]
    return jnp.concatenate(
        [first * cosine - second * sine, second * cosine + first * sine], axis=-1
    )


def attend(query_block, query_raw, query_pos, window_k, window_v, key_raw, key_pos, key_live):
    count = window_k.shape[0]
    kv_heads = window_k.shape[1] // HEAD_DIMENSION
    head_group = query_block.shape[2]
    tile = math.gcd(512, count)
    turns = count // tile
    items = (
        window_k.reshape(turns, tile, kv_heads, HEAD_DIMENSION),
        window_v.reshape(turns, tile, kv_heads, HEAD_DIMENSION),
        key_raw.reshape(turns, tile),
        key_pos.reshape(turns, tile),
        key_live.reshape(turns, tile),
    )

    def visit(carry, item):
        numerator, total = carry
        tile_k, tile_v, tile_raw, tile_pos, tile_live = item
        score = jnp.einsum(
            "qhgd,khd->hgqk", query_block, tile_k, preferred_element_type=jnp.float32
        )
        capped = softcap_limit * jnp.tanh(score / softcap_limit)
        allowed = (
            tile_live[None, :]
            & (tile_raw[None, :] <= query_raw[:, None])
            & (query_pos[:, None] - tile_pos[None, :] < WINDOW)
        )
        weight = jnp.where(allowed[None, None], jnp.exp(capped), jnp.float32(0.0))
        total = total + jnp.sum(weight, axis=-1)
        numerator = numerator + jnp.einsum(
            "nexi,inv->xnev",
            weight.astype(jnp.bfloat16),
            tile_v,
            preferred_element_type=jnp.float32,
        )
        return ((numerator, total), None)

    rows_q = query_block.shape[0]
    start_numer = jnp.zeros((rows_q, kv_heads, head_group, HEAD_DIMENSION), jnp.float32)
    start_total = jnp.zeros((kv_heads, head_group, rows_q), jnp.float32)
    (numerator, total), unused = lax.scan(visit, (start_numer, start_total), items)
    return (numerator, total)


def body(queries, keys, values, dirty, spans):
    every_span, every_dirty = (
        lax.all_gather(spans, "seq", axis=0, tiled=True),
        lax.all_gather(dirty, "seq", axis=0, tiled=True),
    )
    shard_index = lax.axis_index("seq")
    rows = keys.shape[0]
    columns = keys.shape[1]
    kv_heads = columns // HEAD_DIMENSION
    q_heads = queries.shape[1] // HEAD_DIMENSION
    head_group = q_heads // kv_heads
    back = WINDOW // rows + 1
    own_raw = shard_index * rows + jnp.arange(rows)
    own_pos, own_live = locate(own_raw, every_span)
    key_rot = apply_rotary(
        keys.astype(jnp.float32).reshape(rows, kv_heads, HEAD_DIMENSION),
        own_pos.astype(jnp.float32),
    )
    key_rot = key_rot.astype(jnp.bfloat16).reshape(rows, columns)
    block = every_dirty[shard_index]
    chosen = jnp.maximum(block, 0)
    q_raw = shard_index * rows + chosen * BLOCK_ROWS + jnp.arange(BLOCK_ROWS)
    q_pos, q_live = locate(q_raw, every_span)
    query_rotary = (
        apply_rotary(
            queries.astype(jnp.float32).reshape(BLOCK_ROWS, q_heads, HEAD_DIMENSION),
            q_pos.astype(jnp.float32),
        )
        * query_scale
    )
    query_rotary = query_rotary.astype(jnp.bfloat16).reshape(
        BLOCK_ROWS, kv_heads, head_group, HEAD_DIMENSION
    )
    numerator, total = attend(
        query_rotary, q_raw, q_pos, key_rot, values, own_raw, own_pos, own_live
    )
    last = lax.axis_size("seq") - 1
    for step in range(1, back + 1):
        visitor = from_behind(query_rotary, "seq", -step)
        asking = jnp.minimum(shard_index + step, last)
        asking_block = jnp.maximum(every_dirty[asking], 0)
        asking_raw = asking * rows + asking_block * BLOCK_ROWS + jnp.arange(BLOCK_ROWS)
        asking_pos, unused_live = locate(asking_raw, every_span)
        part_numer, part_total = attend(
            visitor, asking_raw, asking_pos, key_rot, values, own_raw, own_pos, own_live
        )
        back_numer, back_total = from_behind((part_numer, part_total), "seq", step)
        numerator = numerator + back_numer
        total = total + back_total
    total = jnp.where(total > 0, total, jnp.float32(1.0))
    result = numerator / jnp.transpose(total, (2, 0, 1))[..., None]
    keep = q_live & (block >= 0)
    result = jnp.where(keep[:, None, None, None], result, jnp.float32(0.0))
    return result.reshape(BLOCK_ROWS, q_heads * HEAD_DIMENSION).astype(jnp.bfloat16)


def solution(mesh):
    placed = (
        P(("groups", "seq"), None),
        P(("groups", "seq"), None),
        P(("groups", "seq"), None),
        P(("groups", "seq")),
        P(("groups", "seq"), None),
    )
    return jax.shard_map(
        body, mesh=mesh, in_specs=placed, out_specs=P(("groups", "seq"), None), check_vma=False
    )
```

profile of v0, /device:TPU:28, one launch (start us, length us, event | category | flops | bytes accessed | tf_op | source)
XLA Modules:
  0.0 487.1 jit_solution(8376926354485233773)
XLA Ops:
  0.0 16.9 %all-gather = s32[16,1,2]{2,1,0:T(1,128)S(1)} all-gather(s32[1,1,2]{2,1,0:T(1,128)} %bitcast.319), channel_id=1, replica_groups=mesh['groups'=2,'seq'=16] {'seq'}, dimensions={0}, use_global_device_ids=true | all-gather | bytes 136 | tf_op jit(solution)/shard_map/all_gather | solution.py:94
  19.7 13.1 %all-reduce = s32[16]{0:T(128)S(1)} all-reduce(s32[16]{0:T(128)S(1)} %dynamic-update-slice), channel_id=1, replica_groups=mesh['groups'=2,'seq'=16] {'seq'}, use_global_device_ids=true, to_apply=%add | all-reduce | flops 16 | bytes 128
  79.4 32.4 %while.79 = (s32[]{:T(128)}, f32[256,8,2,128]{0,3,2,1:T(8,128)}, f32[8,2,256]{2,1,0:T(2,128)}, bf16[2,512,8,128]{1,3,2,0:T(8,128)(2,1)}, pred[2,512]{1,0:T(4,128...) while((s32[]{:T(128)}, f32[256,8,2,128]{0,3,2,1:T(8,128)}, ...), condition=%wide.region_10.11_spmd.clone, body=%wide.region_8.10_spmd.clone.sunk | while | flops 1092227328 | bytes 32982192 | solution.py:88
  79.8 7.3 %fusion.179 = (f32[8,2,256]{2,1,0:T(2,128)S(1)}, f32[8,512,256,2]{2,1,3,0:T(8,128)}) fusion(pred[256,512]{0,1:T(8,128)(4,1)S(1)} %fusion.178, bf16[256,8,2,128]{3,0,2,1:T(8,128)(2,1)} %get-tuple-element.1670, bf16[2,512,8,128]{3,1,2,0:T(8,128)(2,1)} %get-tuple-element.1669, s32[]{:T(128)} %get-tuple-element.1648), kind=kOutput, calls=%fused_computation.30.clone.1 | convolution fusion | flops 545255424 | bytes 10633728 | tf_op jit(solution)/shard_map/while/body/eval_jaxpr/qhgd,khd->hgqk/dot_general | solution.py:66
  95.3 7.3 %fusion.179 = (f32[8,2,256]{2,1,0:T(2,128)S(1)}, f32[8,512,256,2]{2,1,3,0:T(8,128)}) fusion(pred[256,512]{0,1:T(8,128)(4,1)S(1)} %fusion.178, bf16[256,8,2,128]{3,0,2,1:T(8,128)(2,1)} %get-tuple-element.1670, bf16[2,512,8,128]{3,1,2,0:T(8,128)(2,1)} %get-tuple-element.1669, s32[]{:T(128)} %get-tuple-element.1648), kind=kOutput, calls=%fused_computation.30.clone.1 | convolution fusion | flops 545255424 | bytes 10633728 | tf_op jit(solution)/shard_map/while/body/eval_jaxpr/qhgd,khd->hgqk/dot_general | solution.py:66
  102.6 7.9 %bitcast_add_fusion.13 = f32[256,8,2,128]{0,3,2,1:T(8,128)} fusion(f32[256,8,2,128]{0,3,2,1:T(8,128)} %get-tuple-element.1649, f32[8,512,256,2]{2,1,3,0:T(8,128)} %get-tuple-element.1378, pred[256,512]{0,1:T(8,128)(4,1)S(1)} %fusion.178, bf16[2,512,8,128]{1,3,2,0:T(8,128)(2,1)S(1)} %copy-done.1, s32[]{:T(128)} %get-tuple-element.1648, pred[]{:T(512)S(6)} %compare.19), kind=kOutput, calls=%fused_computation.34.clone.1 | convolution fusion | flops 546308096 | bytes 13762565 | tf_op jit(solution)/shard_map/while/body/eval_jaxpr/nexi,inv->xnev/dot_general | solution.py:77
  114.4 30.7 %while.80 = (s32[]{:T(128)}, f32[256,8,2,128]{0,3,2,1:T(8,128)}, f32[8,2,256]{2,1,0:T(2,128)S(1)}, bf16[2,512,8,128]{1,3,2,0:T(8,128)(2,1)}, pred[2,512]{1,0:T(4...) while((s32[]{:T(128)}, f32[256,8,2,128]{0,3,2,1:T(8,128)}, ...), condition=%wide.region_14.15_spmd.clone, body=%wide.region_12.14_spmd.clone.sunk | while | flops 1092227328 | bytes 32982192 | solution.py:88
  137.3 7.9 %bitcast_add_fusion.14 = f32[256,8,2,128]{0,3,2,1:T(8,128)} fusion(f32[256,8,2,128]{0,3,2,1:T(8,128)} %get-tuple-element.1571, f32[8,512,256,2]{2,1,3,0:T(8,128)} %get-tuple-element.1393, pred[256,512]{0,1:T(8,128)(4,1)S(1)} %fusion.183, bf16[2,512,8,128]{1,3,2,0:T(8,128)(2,1)S(1)} %copy-done.2, s32[]{:T(128)} %get-tuple-element.1570, pred[]{:T(512)S(6)} %compare.20), kind=kOutput, calls=%fused_computation.57.clone.1 | convolution fusion | flops 546308096 | bytes 13762565 | tf_op jit(solution)/shard_map/while/body/eval_jaxpr/nexi,inv->xnev/dot_general | solution.py:77
  148.4 30.6 %while.81 = (s32[]{:T(128)}, f32[256,8,2,128]{0,3,2,1:T(8,128)}, f32[8,2,256]{2,1,0:T(2,128)S(1)}, bf16[2,512,8,128]{1,3,2,0:T(8,128)(2,1)}, pred[2,512]{1,0:T(4...) while((s32[]{:T(128)}, f32[256,8,2,128]{0,3,2,1:T(8,128)}, ...), condition=%wide.region_18.19_spmd.clone, body=%wide.region_16.18_spmd.clone.sunk | while | flops 1092227328 | bytes 32982192 | solution.py:88
  148.8 7.3 %fusion.189 = (f32[8,2,256]{2,1,0:T(2,128)S(1)}, f32[8,512,256,2]{2,1,3,0:T(8,128)}) fusion(pred[256,512]{0,1:T(8,128)(4,1)S(1)} %fusion.188, bf16[256,8,2,128]{3,0,2,1:T(8,128)(2,1)} %get-tuple-element.1553, bf16[2,512,8,128]{3,1,2,0:T(8,128)(2,1)} %get-tuple-element.1552, s32[]{:T(128)} %get-tuple-element.1531), kind=kOutput, calls=%fused_computation.76.clone.1 | convolution fusion | flops 545255424 | bytes 10633728 | tf_op jit(solution)/shard_map/while/body/eval_jaxpr/qhgd,khd->hgqk/dot_general | solution.py:66
  156.1 7.3 %bitcast_add_fusion.15 = f32[256,8,2,128]{0,3,2,1:T(8,128)} fusion(f32[256,8,2,128]{0,3,2,1:T(8,128)} %get-tuple-element.1532, f32[8,512,256,2]{2,1,3,0:T(8,128)} %get-tuple-element.1408, pred[256,512]{0,1:T(8,128)(4,1)S(1)} %fusion.188, bf16[2,512,8,128]{1,3,2,0:T(8,128)(2,1)S(1)} %copy-done.3, s32[]{:T(128)} %get-tuple-element.1531, pred[]{:T(512)S(6)} %compare.21), kind=kOutput, calls=%fused_computation.80.clone.1 | convolution fusion | flops 546308096 | bytes 13762565 | tf_op jit(solution)/shard_map/while/body/eval_jaxpr/nexi,inv->xnev/dot_general | solution.py:77
  163.8 7.3 %fusion.189 = (f32[8,2,256]{2,1,0:T(2,128)S(1)}, f32[8,512,256,2]{2,1,3,0:T(8,128)}) fusion(pred[256,512]{0,1:T(8,128)(4,1)S(1)} %fusion.188, bf16[256,8,2,128]{3,0,2,1:T(8,128)(2,1)} %get-tuple-element.1553, bf16[2,512,8,128]{3,1,2,0:T(8,128)(2,1)} %get-tuple-element.1552, s32[]{:T(128)} %get-tuple-element.1531), kind=kOutput, calls=%fused_computation.76.clone.1 | convolution fusion | flops 545255424 | bytes 10633728 | tf_op jit(solution)/shard_map/while/body/eval_jaxpr/qhgd,khd->hgqk/dot_general | solution.py:66
  171.1 7.9 %bitcast_add_fusion.15 = f32[256,8,2,128]{0,3,2,1:T(8,128)} fusion(f32[256,8,2,128]{0,3,2,1:T(8,128)} %get-tuple-element.1532, f32[8,512,256,2]{2,1,3,0:T(8,128)} %get-tuple-element.1408, pred[256,512]{0,1:T(8,128)(4,1)S(1)} %fusion.188, bf16[2,512,8,128]{1,3,2,0:T(8,128)(2,1)S(1)} %copy-done.3, s32[]{:T(128)} %get-tuple-element.1531, pred[]{:T(512)S(6)} %compare.21), kind=kOutput, calls=%fused_computation.80.clone.1 | convolution fusion | flops 546308096 | bytes 13762565 | tf_op jit(solution)/shard_map/while/body/eval_jaxpr/nexi,inv->xnev/dot_general | solution.py:77
  181.0 31.0 %while.82 = (s32[]{:T(128)}, f32[256,8,2,128]{0,3,2,1:T(8,128)}, f32[8,2,256]{2,1,0:T(2,128)S(1)}, bf16[2,512,8,128]{1,3,2,0:T(8,128)(2,1)}, pred[2,512]{1,0:T(4...) while((s32[]{:T(128)}, f32[256,8,2,128]{0,3,2,1:T(8,128)}, ...), condition=%wide.region_22.23_spmd.clone, body=%wide.region_20.22_spmd.clone.sunk | while | flops 1092227328 | bytes 32982192 | solution.py:88
  181.8 7.3 %fusion.194 = (f32[8,2,256]{2,1,0:T(2,128)S(1)}, f32[8,512,256,2]{2,1,3,0:T(8,128)}) fusion(pred[256,512]{0,1:T(8,128)(4,1)S(1)} %fusion.193, bf16[256,8,2,128]{3,0,2,1:T(8,128)(2,1)} %get-tuple-element.1514, bf16[2,512,8,128]{3,1,2,0:T(8,128)(2,1)} %get-tuple-element.1513, s32[]{:T(128)} %get-tuple-element.1492), kind=kOutput, calls=%fused_computation.99.clone.1 | convolution fusion | flops 545255424 | bytes 10633728 | tf_op jit(solution)/shard_map/while/body/eval_jaxpr/qhgd,khd->hgqk/dot_general | solution.py:66
  204.1 7.9 %bitcast_add_fusion.16 = f32[256,8,2,128]{0,3,2,1:T(8,128)} fusion(f32[256,8,2,128]{0,3,2,1:T(8,128)} %get-tuple-element.1493, f32[8,512,256,2]{2,1,3,0:T(8,128)} %get-tuple-element.1423, pred[256,512]{0,1:T(8,128)(4,1)S(1)} %fusion.193, bf16[2,512,8,128]{1,3,2,0:T(8,128)(2,1)S(1)} %copy-done.4, s32[]{:T(128)} %get-tuple-element.1492, pred[]{:T(512)S(6)} %compare.22), kind=kOutput, calls=%fused_computation.103.clone.1 | convolution fusion | flops 546308096 | bytes 13762565 | tf_op jit(solution)/shard_map/while/body/eval_jaxpr/nexi,inv->xnev/dot_general | solution.py:77
  213.4 30.6 %while.83 = (s32[]{:T(128)}, f32[256,8,2,128]{0,3,2,1:T(8,128)}, f32[8,2,256]{2,1,0:T(2,128)S(1)}, bf16[2,512,8,128]{1,3,2,0:T(8,128)(2,1)}, pred[2,512]{1,0:T(4...) while((s32[]{:T(128)}, f32[256,8,2,128]{0,3,2,1:T(8,128)}, ...), condition=%wide.region_26.27_spmd.clone, body=%wide.region_24.26_spmd.clone.sunk | while | flops 1092227328 | bytes 32982192 | solution.py:88
  221.0 7.3 %bitcast_add_fusion.17 = f32[256,8,2,128]{0,3,2,1:T(8,128)} fusion(f32[256,8,2,128]{0,3,2,1:T(8,128)} %get-tuple-element.1454, f32[8,512,256,2]{2,1,3,0:T(8,128)} %get-tuple-element.1438, pred[256,512]{0,1:T(8,128)(4,1)S(1)} %fusion.198, bf16[2,512,8,128]{1,3,2,0:T(8,128)(2,1)S(1)} %copy-done.5, s32[]{:T(128)} %get-tuple-element.1453, pred[]{:T(512)S(6)} %compare.23), kind=kOutput, calls=%fused_computation.126.clone.1 | convolution fusion | flops 546308096 | bytes 13762565 | tf_op jit(solution)/shard_map/while/body/eval_jaxpr/nexi,inv->xnev/dot_general | solution.py:77
  236.0 7.9 %bitcast_add_fusion.17 = f32[256,8,2,128]{0,3,2,1:T(8,128)} fusion(f32[256,8,2,128]{0,3,2,1:T(8,128)} %get-tuple-element.1454, f32[8,512,256,2]{2,1,3,0:T(8,128)} %get-tuple-element.1438, pred[256,512]{0,1:T(8,128)(4,1)S(1)} %fusion.198, bf16[2,512,8,128]{1,3,2,0:T(8,128)(2,1)S(1)} %copy-done.5, s32[]{:T(128)} %get-tuple-element.1453, pred[]{:T(512)S(6)} %compare.23), kind=kOutput, calls=%fused_computation.126.clone.1 | convolution fusion | flops 546308096 | bytes 13762565 | tf_op jit(solution)/shard_map/while/body/eval_jaxpr/nexi,inv->xnev/dot_general | solution.py:77
  253.8 30.7 %while.78 = (s32[]{:T(128)}, f32[256,8,2,128]{0,3,2,1:T(8,128)}, f32[8,2,256]{2,1,0:T(2,128)S(1)}, bf16[2,512,8,128]{1,3,2,0:T(8,128)(2,1)}, pred[2,512]{1,0:T(4...) while((s32[]{:T(128)}, f32[256,8,2,128]{0,3,2,1:T(8,128)}, ...), condition=%wide.region_6.7_spmd.clone, body=%wide.region_4.6_spmd.clone.sunk | while | flops 1092227328 | bytes 32982192 | solution.py:88
  276.6 7.9 %bitcast_add_fusion.12 = f32[256,8,2,128]{0,3,2,1:T(8,128)} fusion(f32[256,8,2,128]{0,3,2,1:T(8,128)} %get-tuple-element.1610, f32[8,512,256,2]{2,1,3,0:T(8,128)} %get-tuple-element.1363, pred[256,512]{0,1:T(8,128)(4,1)S(1)} %fusion.173, bf16[2,512,8,128]{1,3,2,0:T(8,128)(2,1)S(1)} %copy-done.6, s32[]{:T(128)} %get-tuple-element.1609, pred[]{:T(512)S(6)} %compare.18), kind=kOutput, calls=%fused_computation.11.clone.1 | convolution fusion | flops 546308096 | bytes 13762565 | tf_op jit(solution)/shard_map/while/body/eval_jaxpr/nexi,inv->xnev/dot_general | solution.py:77
  285.9 7.5 %collective-permute-done.1 = f32[256,8,2,128]{0,3,2,1:T(8,128)} collective-permute-done((f32[256,8,2,128]{0,3,2,1:T(8,128)}, f32[256,8,2,128]{0,3,2,1:T(8,128)}, u32[]{:S(2)}, u32[]{:S(2)}) %collective-permute-start.1) | collective-permute-done | bytes 2097184 | tf_op jit(solution)/shard_map/ppermute | solution.py:20
  299.6 37.6 %collective-permute-done.5 = f32[256,8,2,128]{0,3,2,1:T(8,128)} collective-permute-done((f32[256,8,2,128]{0,3,2,1:T(8,128)}, f32[256,8,2,128]{0,3,2,1:T(8,128)}, u32[]{:S(2)}, u32[]{:S(2)}) %collective-permute-start.5) | collective-permute-done | bytes 2097184 | tf_op jit(solution)/shard_map/ppermute | solution.py:20
  337.3 142.2 %collective-permute-done.9 = f32[256,8,2,128]{0,3,2,1:T(8,128)} collective-permute-done((f32[256,8,2,128]{0,3,2,1:T(8,128)}, f32[256,8,2,128]{0,3,2,1:T(8,128)}, u32[]{:S(2)}, u32[]{:S(2)}) %collective-permute-start.9) | collective-permute-done | bytes 2097184 | tf_op jit(solution)/shard_map/ppermute | solution.py:20
  (189 shorter events, 164.0 us)
Async XLA Ops:
  42.8 14.7 %copy-start = (bf16[1024,1024]{1,0:T(8,128)(2,1)S(1)}, bf16[1024,1024]{1,0:T(8,128)(2,1)}, u32[]{:S(2)}) copy-start(bf16[1024,1024]{1,0:T(8,128)(2,1)} %param.18) | copy-start | bytes 6291460
  44.4 35.0 %collective-permute-start = (bf16[256,8,2,128]{3,0,2,1:T(8,128)(2,1)}, bf16[256,8,2,128]{3,0,2,1:T(8,128)(2,1)}, u32[]{:S(2)}, u32[]{:S(2)}) collective-permute-start(bf16[256,8,2,128]{3,0,2,1:T(8,128)(2,1)} %fusion.120), channel_id=1, source_target_pairs={{1,0},{2,1},{3,2},{4,3},{5,4},{6,5},{7,6},{8,7},{9,8},{10,9},{11,1... | collective-permute-start | bytes 3145736 | tf_op jit(solution)/shard_map/ppermute | solution.py:20
  46.4 68.1 %collective-permute-start.2 = (bf16[256,8,2,128]{3,0,2,1:T(8,128)(2,1)}, bf16[256,8,2,128]{3,0,2,1:T(8,128)(2,1)}, u32[]{:S(2)}, u32[]{:S(2)}) collective-permute-start(bf16[256,8,2,128]{3,0,2,1:T(8,128)(2,1)} %fusion.120), channel_id=1, source_target_pairs={{2,0},{3,1},{4,2},{5,3},{6,4},{7,5},{8,6},{9,7},{10,8},{11,9},{12,... | collective-permute-start | bytes 3145736 | tf_op jit(solution)/shard_map/ppermute | solution.py:20
  48.3 100.2 %collective-permute-start.4 = (bf16[256,8,2,128]{3,0,2,1:T(8,128)(2,1)}, bf16[256,8,2,128]{3,0,2,1:T(8,128)(2,1)}, u32[]{:S(2)}, u32[]{:S(2)}) collective-permute-start(bf16[256,8,2,128]{3,0,2,1:T(8,128)(2,1)} %fusion.120), channel_id=1, source_target_pairs={{3,0},{4,1},{5,2},{6,3},{7,4},{8,5},{9,6},{10,7},{11,8},{12,9},{13... | collective-permute-start | bytes 3145736 | tf_op jit(solution)/shard_map/ppermute | solution.py:20
  50.9 130.1 %collective-permute-start.6 = (bf16[256,8,2,128]{3,0,2,1:T(8,128)(2,1)}, bf16[256,8,2,128]{3,0,2,1:T(8,128)(2,1)}, u32[]{:S(2)}, u32[]{:S(2)}) collective-permute-start(bf16[256,8,2,128]{3,0,2,1:T(8,128)(2,1)} %fusion.120), channel_id=1, source_target_pairs={{4,0},{5,1},{6,2},{7,3},{8,4},{9,5},{10,6},{11,7},{12,8},{13,9},{1... | collective-permute-start | bytes 3145736 | tf_op jit(solution)/shard_map/ppermute | solution.py:20
  54.0 159.3 %collective-permute-start.8 = (bf16[256,8,2,128]{3,0,2,1:T(8,128)(2,1)}, bf16[256,8,2,128]{3,0,2,1:T(8,128)(2,1)}, u32[]{:S(2)}, u32[]{:S(2)}) collective-permute-start(bf16[256,8,2,128]{3,0,2,1:T(8,128)(2,1)} %fusion.120), channel_id=1, source_target_pairs={{5,0},{6,1},{7,2},{8,3},{9,4},{10,5},{11,6},{12,7},{13,8},{14,9},{... | collective-permute-start | bytes 3145736 | tf_op jit(solution)/shard_map/ppermute | solution.py:20
  79.8 7.3 %copy-start.1 = (bf16[2,512,8,128]{1,3,2,0:T(8,128)(2,1)S(1)}, bf16[2,512,8,128]{1,3,2,0:T(8,128)(2,1)}, u32[]{:S(2)}) copy-start(bf16[2,512,8,128]{1,3,2,0:T(8,128)(2,1)} %get-tuple-element.1664) | copy-start | bytes 6291460 | tf_op jit(solution)/shard_map/while
  111.8 133.5 %collective-permute-start.10 = (f32[8,2,256]{2,1,0:T(2,128)}, f32[8,2,256]{2,1,0:T(2,128)}, u32[]{:S(2)}, u32[]{:S(2)}) collective-permute-start(f32[8,2,256]{2,1,0:T(2,128)} %get-tuple-element.360), channel_id=1, source_target_pairs={{0,1},{1,2},{2,3},{3,4},{4,5},{5,6},{6,7},{7,8},{8,9},{9,10},{10,1... | collective-permute-start | bytes 49160 | tf_op jit(solution)/shard_map/ppermute | solution.py:20
  145.2 102.1 %collective-permute-start.11 = (f32[8,2,256]{2,1,0:T(2,128)S(1)}, f32[8,2,256]{2,1,0:T(2,128)S(1)}, u32[]{:S(2)}, u32[]{:S(2)}) collective-permute-start(f32[8,2,256]{2,1,0:T(2,128)S(1)} %get-tuple-element.361), channel_id=1, source_target_pairs={{0,2},{1,3},{2,4},{3,5},{4,6},{5,7},{6,8},{7,9},{8,10},{9,11},{10,... | collective-permute-start | bytes 49160 | tf_op jit(solution)/shard_map/ppermute | solution.py:20
  148.8 7.3 %copy-start.3 = (bf16[2,512,8,128]{1,3,2,0:T(8,128)(2,1)S(1)}, bf16[2,512,8,128]{1,3,2,0:T(8,128)(2,1)}, u32[]{:S(2)}) copy-start(bf16[2,512,8,128]{1,3,2,0:T(8,128)(2,1)} %get-tuple-element.1547) | copy-start | bytes 6291460 | tf_op jit(solution)/shard_map/while
  163.8 7.3 %copy-start.3 = (bf16[2,512,8,128]{1,3,2,0:T(8,128)(2,1)S(1)}, bf16[2,512,8,128]{1,3,2,0:T(8,128)(2,1)}, u32[]{:S(2)}) copy-start(bf16[2,512,8,128]{1,3,2,0:T(8,128)(2,1)} %get-tuple-element.1547) | copy-start | bytes 6291460 | tf_op jit(solution)/shard_map/while
  179.1 70.1 %collective-permute-start.12 = (f32[8,2,256]{2,1,0:T(2,128)S(1)}, f32[8,2,256]{2,1,0:T(2,128)S(1)}, u32[]{:S(2)}, u32[]{:S(2)}) collective-permute-start(f32[8,2,256]{2,1,0:T(2,128)S(1)} %get-tuple-element.362), channel_id=1, source_target_pairs={{0,3},{1,4},{2,5},{3,6},{4,7},{5,8},{6,9},{7,10},{8,11},{9,12},{10... | collective-permute-start | bytes 49160 | tf_op jit(solution)/shard_map/ppermute | solution.py:20
  181.0 32.3 %copy-start.7 = (f32[8,2,256]{2,1,0:T(2,128)S(1)}, f32[8,2,256]{2,1,0:T(2,128)}, u32[]{:S(2)}) copy-start(f32[8,2,256]{2,1,0:T(2,128)} %custom-call.11) | copy-start | bytes 49156
  181.0 32.3 %copy-start.9 = (s32[256]{0:T(256)S(1)}, s32[256]{0:T(256)}, u32[]{:S(2)}) copy-start(s32[256]{0:T(256)} %fusion.128) | copy-start | bytes 3076
  181.8 7.3 %copy-start.4 = (bf16[2,512,8,128]{1,3,2,0:T(8,128)(2,1)S(1)}, bf16[2,512,8,128]{1,3,2,0:T(8,128)(2,1)}, u32[]{:S(2)}) copy-start(bf16[2,512,8,128]{1,3,2,0:T(8,128)(2,1)} %get-tuple-element.1508) | copy-start | bytes 6291460 | tf_op jit(solution)/shard_map/while
  212.0 39.1 %collective-permute-start.13 = (f32[8,2,256]{2,1,0:T(2,128)S(1)}, f32[8,2,256]{2,1,0:T(2,128)S(1)}, u32[]{:S(2)}, u32[]{:S(2)}) collective-permute-start(f32[8,2,256]{2,1,0:T(2,128)S(1)} %get-tuple-element.363), channel_id=1, source_target_pairs={{0,4},{1,5},{2,6},{3,7},{4,8},{5,9},{6,10},{7,11},{8,12},{9,13},{1... | collective-permute-start | bytes 49160 | tf_op jit(solution)/shard_map/ppermute | solution.py:20
  213.3 40.4 %copy-start.8 = (s32[256]{0:T(256)S(1)}, s32[256]{0:T(256)}, u32[]{:S(2)}) copy-start(s32[256]{0:T(256)} %get-tuple-element.1602) | copy-start | bytes 3076
  244.0 8.5 %collective-permute-start.14 = (f32[8,2,256]{2,1,0:T(2,128)S(1)}, f32[8,2,256]{2,1,0:T(2,128)S(1)}, u32[]{:S(2)}, u32[]{:S(2)}) collective-permute-start(f32[8,2,256]{2,1,0:T(2,128)S(1)} %get-tuple-element.364), channel_id=1, source_target_pairs={{0,5},{1,6},{2,7},{3,8},{4,9},{5,10},{6,11},{7,12},{8,13},{9,14},{... | collective-permute-start | bytes 49160 | tf_op jit(solution)/shard_map/ppermute | solution.py:20
  245.3 48.0 %collective-permute-start.1 = (f32[256,8,2,128]{0,3,2,1:T(8,128)}, f32[256,8,2,128]{0,3,2,1:T(8,128)}, u32[]{:S(2)}, u32[]{:S(2)}) collective-permute-start(f32[256,8,2,128]{0,3,2,1:T(8,128)} %get-tuple-element.354), channel_id=1, source_target_pairs={{0,1},{1,2},{2,3},{3,4},{4,5},{5,6},{6,7},{7,8},{8,9},{9,10},{10,1... | collective-permute-start | bytes 6291464 | tf_op jit(solution)/shard_map/ppermute | solution.py:20
  247.3 52.4 %collective-permute-start.3 = (f32[256,8,2,128]{0,3,2,1:T(8,128)}, f32[256,8,2,128]{0,3,2,1:T(8,128)}, u32[]{:S(2)}, u32[]{:S(2)}) collective-permute-start(f32[256,8,2,128]{0,3,2,1:T(8,128)} %get-tuple-element.355), channel_id=1, source_target_pairs={{0,2},{1,3},{2,4},{3,5},{4,6},{5,7},{6,8},{7,9},{8,10},{9,11},{10,... | collective-permute-start | bytes 6291464 | tf_op jit(solution)/shard_map/ppermute | solution.py:20
  249.2 88.1 %collective-permute-start.5 = (f32[256,8,2,128]{0,3,2,1:T(8,128)}, f32[256,8,2,128]{0,3,2,1:T(8,128)}, u32[]{:S(2)}, u32[]{:S(2)}) collective-permute-start(f32[256,8,2,128]{0,3,2,1:T(8,128)} %get-tuple-element.356), channel_id=1, source_target_pairs={{0,3},{1,4},{2,5},{3,6},{4,7},{5,8},{6,9},{7,10},{8,11},{9,12},{10... | collective-permute-start | bytes 6291464 | tf_op jit(solution)/shard_map/ppermute | solution.py:20
  251.1 86.1 %collective-permute-start.7 = (f32[256,8,2,128]{0,3,2,1:T(8,128)}, f32[256,8,2,128]{0,3,2,1:T(8,128)}, u32[]{:S(2)}, u32[]{:S(2)}) collective-permute-start(f32[256,8,2,128]{0,3,2,1:T(8,128)} %get-tuple-element.357), channel_id=1, source_target_pairs={{0,4},{1,5},{2,6},{3,7},{4,8},{5,9},{6,10},{7,11},{8,12},{9,13},{1... | collective-permute-start | bytes 6291464 | tf_op jit(solution)/shard_map/ppermute | solution.py:20
  252.5 227.1 %collective-permute-start.9 = (f32[256,8,2,128]{0,3,2,1:T(8,128)}, f32[256,8,2,128]{0,3,2,1:T(8,128)}, u32[]{:S(2)}, u32[]{:S(2)}) collective-permute-start(f32[256,8,2,128]{0,3,2,1:T(8,128)} %get-tuple-element.358), channel_id=1, source_target_pairs={{0,5},{1,6},{2,7},{3,8},{4,9},{5,10},{6,11},{7,12},{8,13},{9,14},{... | collective-permute-start | bytes 6291464 | tf_op jit(solution)/shard_map/ppermute | solution.py:20
  253.8 31.4 %copy-start.10 = (s32[256]{0:T(256)S(1)}, s32[256]{0:T(256)}, u32[]{:S(2)}) copy-start(s32[256]{0:T(256)} %get-tuple-element.799) | copy-start | bytes 3076
  (8 other events, 58.5 us)
where the time goes:
time: 493 us; the launch traced here: 487 us
  waiting for transfers between devices  194 us (39%)
  matrix products  179 us (36%)
  starting transfers between devices  30.6 us (6%)
  blocking collectives  30 us (6%)
  other arithmetic  26.7 us (5%)
  local copies, waits for them, and re-layouts  20.1 us (4%)
  between operations  5.9 us (1%)
    ppermute x15, waiting for transfers between devices, from_behind(): return lax.ppermute(array, axis, pairs)  194 us
    dot_general x12, matrix products, visit(): jnp.einsum('nexi,inv->xnev', weight.astype(jnp.bfloat16), tile_v, preferr...  91.1 us
    dot_general x12, matrix products, visit(): jnp.einsum('qhgd,khd->hgqk', query_block, tile_k, preferred_element_type=...  87.7 us
    ppermute x15, starting transfers between devices, from_behind(): return lax.ppermute(array, axis, pairs)  30.6 us
    all_gather x1, blocking collectives, body(): lax.all_gather(spans, 'seq', axis=0, tiled=True)  16.9 us
    unnamed x1, blocking collectives  13.1 us
    unnamed x17, local copies, waits for them, and re-layouts  11.2 us
  transfers between devices with their start and end apart: 15, of which 4 were waited for; matrix products, arithmetic and copies ran while one was open for 43% of the time, Pallas kernels for 0%

commit v1 on v0

v1 whole, which is shorter than its diff:
```python
import functools
import math

import jax
import jax.numpy as jnp
import numpy as np
from jax import lax
from jax.experimental import pallas as pl
from jax.experimental.pallas import tpu as pltpu
from jax.sharding import PartitionSpec as P


HEAD_DIMENSION = 128
WINDOW = 4096
BLOCK_ROWS = 256
SPAN = 32

SOFTCAP = 50.0
QUERY_SCALE = 144.0 ** (-0.5)
TO_TANH = 1.0 / SOFTCAP
TO_EXP2 = SOFTCAP * math.log2(math.e)

HALF = HEAD_DIMENSION // 2
LANES = 128
NOTE_ROWS = 8
DIGIT = 32
VMEM_LIMIT = 32 << 20


def lane_frequency():
    order = np.arange(HEAD_DIMENSION) % HALF
    return np.exp(order * (-2.0 * math.log(10000.0) / HEAD_DIMENSION)).astype(np.float32)


def row_angles():
    angle = np.arange(BLOCK_ROWS, dtype=np.float64)[:, None] * lane_frequency().astype(np.float64)[None, :]
    sign = np.where(np.arange(HEAD_DIMENSION) < HALF, -1.0, 1.0)[None, :]
    return np.stack([np.cos(angle), np.sin(angle) * sign]).astype(np.float32)


def send(array, pairs):
    return lax.ppermute(array, "seq", pairs)


def shift(array, by):
    count = lax.axis_size("seq")
    return send(array, [(i, i + by) for i in range(count) if 0 <= i + by < count])


class Frame:
    def __init__(self, spans, rows):
        self.spans, self.rows = spans, rows

    def tile(self, shard_step, row):
        start, length = self.spans[shard_step]
        first = shard_step * self.rows + row
        for step in range(min(shard_step, 0), max(shard_step, 0)):
            _, other = self.spans[step]
            first = first - other if step >= 0 else first + other
        first = first - jnp.clip(row - start, 0, length)
        begin = start - row
        end = begin + length
        gone = jnp.clip(end, 0, BLOCK_ROWS) - jnp.clip(begin, 0, BLOCK_ROWS)
        return first, first - gone, begin, end


def by_parity(odd, mine, other):
    mine = [jnp.where(odd == 1, b, a) for a, b in zip(mine, other)], [
        jnp.where(odd == 1, a, b) for a, b in zip(mine, other)
    ]
    return mine


def write_note(ref, numbers):
    shape = (NOTE_ROWS, ref.shape[1])
    lane = lax.broadcasted_iota(jnp.int32, shape, 1)
    row = jnp.zeros(shape, jnp.int32)
    for k, number in enumerate(numbers):
        row = jnp.where(lane == 2 * k, number // DIGIT, jnp.where(lane == 2 * k + 1, number % DIGIT, row))
    ref[ref.shape[0] - NOTE_ROWS :, :] = row.astype(jnp.float32).astype(jnp.bfloat16)


def read_note(ref, count):
    low = ref[ref.shape[0] - NOTE_ROWS :, :LANES].astype(jnp.float32)
    shape = (NOTE_ROWS, LANES)
    lane = lax.broadcasted_iota(jnp.int32, shape, 1)
    first = lax.broadcasted_iota(jnp.int32, shape, 0) == 0
    out = []
    for k in range(count):
        digits = jnp.where(lane == 2 * k, low * DIGIT, jnp.where(lane == 2 * k + 1, low, 0.0))
        out.append(jnp.sum(jnp.where(first, digits, 0.0)).astype(jnp.int32))
    return out


def wave(offsets, freq):
    count = -(-len(offsets) // 8) * 8
    row = lax.broadcasted_iota(jnp.int32, (count, LANES), 0)
    lane = lax.broadcasted_iota(jnp.int32, (count, LANES), 1)
    value = jnp.zeros((count, LANES), jnp.int32)
    for k, offset in enumerate(offsets):
        value = jnp.where(row == k, offset, value)
    angle = value.astype(jnp.float32) * freq
    sine = jnp.sin(angle)
    return jnp.cos(angle), jnp.where(lane < HALF, -sine, sine)


def rope_tables(angles, begin, waves, at, scale):
    cosine, sine = waves
    row = lax.broadcasted_iota(jnp.int32, (BLOCK_ROWS, LANES), 0)
    early = row < begin
    c = jnp.where(early, cosine[at : at + 1], cosine[at + 1 : at + 2])
    s = jnp.where(early, sine[at : at + 1], sine[at + 1 : at + 2])
    rc, rs = angles[0], angles[1]
    return (rc * c - rs * s) * scale, (rs * c + rc * s) * scale


def rotate(x, c, s):
    x = x.astype(jnp.float32)
    return (x * c + pltpu.roll(x, HALF, 1) * s).astype(jnp.bfloat16)


def places(tile, dim, shape):
    first, later, begin, _ = tile
    row = lax.broadcasted_iota(jnp.int32, shape, dim)
    return row + jnp.where(row < begin, first, later)


def visit(kind, index, block, frame, freq, angles, part, query, keys, edge, out, scratch):
    kr, vz, lv = keys
    _, rot, acc, ke, ve, le = scratch
    odd = lax.rem(index, 2)
    per = frame.rows // BLOCK_ROWS
    q_heads = acc.shape[0]
    kv_heads = q_heads // 2
    low = part * kv_heads
    pair = [frame.tile(s, block * BLOCK_ROWS) for s in edge["block"]]
    tile = [jnp.where(odd == 1, b, a) for a, b in zip(*pair)]
    waves = wave([tile[0], tile[1]], freq)
    c, s = rope_tables(angles, tile[2], waves, 0, QUERY_SCALE)
    for head in range(q_heads):
        cols = slice(head * HEAD_DIMENSION, (head + 1) * HEAD_DIMENSION)
        rot[head] = rotate(query[:BLOCK_ROWS, cols], c, s)
    own = places(tile, 0, (BLOCK_ROWS, 1))

    def add(head, keys_of, values_of, keep, fresh):
        score = lax.dot_general(
            rot[head], keys_of, (((1,), (1,)), ((), ())), preferred_element_type=jnp.float32
        )
        weight = jnp.exp2(jnp.tanh(score * TO_TANH) * TO_EXP2)
        if keep is not None:
            weight = jnp.where(keep, weight, 0.0)
        both = jnp.dot(weight.astype(jnp.bfloat16), values_of, preferred_element_type=jnp.float32)
        acc[head] = both if fresh else acc[head] + both

    def many(begin, count, fresh):
        some = pl.ds(pl.multiple_of(begin * BLOCK_ROWS, BLOCK_ROWS), count * BLOCK_ROWS)

        def one(i, carry):
            v = jnp.concatenate([vz[low + i, some, :], lv[some, :]], axis=1)
            for g in range(2):
                add(2 * i + g, kr[low + i, some, :], v, None, fresh)
            return carry

        lax.fori_loop(0, kv_heads, one, 0)

    def single(at, carry):
        some = pl.ds(pl.multiple_of(at * BLOCK_ROWS, BLOCK_ROWS), BLOCK_ROWS)
        live = lv[some, :]
        for i in range(kv_heads):
            v = jnp.concatenate([vz[low + i, some, :], live], axis=1)
            for g in range(2):
                add(2 * i + g, kr[low + i, some, :], v, None, False)
        return carry

    def stage(slot, at):
        some = pl.ds(pl.multiple_of(at * BLOCK_ROWS, BLOCK_ROWS), BLOCK_ROWS)
        for i in range(kv_heads):
            ke[slot, i] = kr[low + i, some, :]
            ve[slot, i] = vz[low + i, some, :]
        le[slot] = lv[some, :]

    def masked(slot, keep, fresh):
        for i in range(kv_heads):
            v = jnp.concatenate([ve[slot, i], le[slot]], axis=1)
            for g in range(2):
                add(2 * i + g, ke[slot, i], v, keep, fresh)

    def places_at(at):
        pair = [frame.tile(s, at * BLOCK_ROWS) for s in (0, 1)]
        tile = [jnp.where(odd == 1, b, a) for a, b in zip(*pair)]
        return places(tile, 1, (1, BLOCK_ROWS))

    if kind == "middle":
        many(0, 2 * per, True)
    elif kind == "own":
        stage(0, odd * per + block)
        masked(0, own >= places_at(block), True)

        @pl.when(odd == 1)
        def _():
            many(0, per, False)

        lax.fori_loop(odd * per, odd * per + block, single, 0)
    else:
        first = odd * per + block
        tail_k, tail_v, tail_tile = edge["tail"]

        @pl.when(first > 0)
        def _():
            stage(0, first - 1)

        @pl.when(first == 0)
        def _():
            reach = tail_k.shape[0]
            row = lax.broadcasted_iota(jnp.int32, (BLOCK_ROWS, LANES), 0)
            live = (row < tail_tile[2]) | (row >= tail_tile[3])
            live = live & (row >= BLOCK_ROWS - reach) & (index > 0)
            c, s = rope_tables(angles, tail_tile[2], wave(list(tail_tile[:2]), freq), 0, 1.0)
            le[0] = jnp.where(live, 1.0, 0.0).astype(jnp.bfloat16)
            zero = jnp.zeros((BLOCK_ROWS - reach, HEAD_DIMENSION), jnp.bfloat16)
            for i in range(kv_heads):
                at = pl.multiple_of((low + i) * HEAD_DIMENSION, HEAD_DIMENSION)
                cols = pl.ds(at, HEAD_DIMENSION)
                ke[0, i] = rotate(jnp.concatenate([zero, tail_k[:, cols]], axis=0), c, s)
                ve[0, i] = jnp.concatenate([zero, tail_v[:, cols]], axis=0) * le[0]

        stage(1, first)
        before = places_at(block - 1)
        before = jnp.where(first == 0, places(tail_tile, 1, (1, BLOCK_ROWS)), before)
        masked(0, own - before < WINDOW, True)
        masked(1, own - places_at(block) < WINDOW, False)

        @pl.when(odd == 0)
        def _():
            many(per, per, False)

        lax.fori_loop(first + 1, (odd + 1) * per, single, 0)

    lane = lax.broadcasted_iota(jnp.int32, (BLOCK_ROWS, LANES), 1)
    sums = jnp.zeros((BLOCK_ROWS, LANES), jnp.float32)
    for head in range(q_heads):
        cols = slice(head * HEAD_DIMENSION, (head + 1) * HEAD_DIMENSION)
        out[:, cols] = acc[head, :, :HEAD_DIMENSION].astype(jnp.bfloat16)
        t = acc[head, :, HEAD_DIMENSION:]
        high = t.astype(jnp.bfloat16).astype(jnp.float32)
        sums = jnp.where(lane == head, high, jnp.where(lane == head + q_heads, t - high, sums))
    out[:, q_heads * HEAD_DIMENSION :] = sums.astype(jnp.bfloat16)


def pack_kernel(spans, other, dirty, keys, values, query, *refs):
    parts = refs[:-2]
    tail, sem = refs[-2:]
    rows = keys.shape[0]
    width = parts[0].shape[1]
    reach = (tail.shape[0] - NOTE_ROWS) // 2
    copies = [
        (query.at[:, p * width : (p + 1) * width], part.at[:BLOCK_ROWS]) for p, part in enumerate(parts)
    ]
    copies += [
        (keys.at[rows - reach :], tail.at[:reach]),
        (values.at[rows - reach :], tail.at[reach : 2 * reach]),
    ]
    copies = [pltpu.make_async_copy(a, b, sem.at[k]) for k, (a, b) in enumerate(copies)]
    for copy in copies:
        copy.start()
    mine = [lax.rem(spans[0, 0], rows), spans[0, 1] - spans[0, 0]]
    write_note(
        parts[0], mine + [lax.rem(other[0, 0], rows), other[0, 1] - other[0, 0], dirty[0] + 1]
    )
    write_note(tail, mine)
    for copy in copies:
        copy.wait()


def chip_spans(index, rows, spans, other):
    mine = [lax.rem(spans[0, 0], rows), spans[0, 1] - spans[0, 0]]
    others = [lax.rem(other[0, 0], rows), other[0, 1] - other[0, 0]]
    return by_parity(lax.rem(index, 2), mine, others)


def prepare_kernel(
    index_ref, spans, other, angles, freq, k_own, k_other, v_own, v_other, kr, vz, lv, kb, vb, waves, sem,
):
    rows = k_own.shape[0]
    per = rows // BLOCK_ROWS
    kv_heads = kr.shape[0]
    index = index_ref[0]
    odd = lax.rem(index, 2)

    def copies(i, pair):
        into = pl.ds(pl.multiple_of(i * BLOCK_ROWS, BLOCK_ROWS), BLOCK_ROWS)
        t = lax.rem(i, per)
        of = pl.ds(pl.multiple_of(t * BLOCK_ROWS, BLOCK_ROWS), BLOCK_ROWS)
        return [
            pltpu.make_async_copy(ref.at[of, :], buf.at[into, :], sem.at[k, i])
            for k, (ref, buf) in enumerate(zip(pair, (kb, vb)))
        ]

    for i in range(2 * per):
        for copy in copies(i, (k_own, v_own) if i < per else (k_other, v_other)):
            copy.start()
    frame = Frame(dict(enumerate(chip_spans(index, rows, spans, other))), rows)
    tiles = [frame.tile(s, t * BLOCK_ROWS) for s in (0, 1) for t in range(per)]
    waves[0], waves[1] = wave([o for tile in tiles for o in tile[:2]], freq[...])
    row = lax.broadcasted_iota(jnp.int32, (BLOCK_ROWS, LANES), 0)

    def one(i, carry):
        for copy in copies(i, (k_own, v_own)):
            copy.wait()
        shard = jnp.where(i < per, odd, 1 - odd)
        t = lax.rem(i, per)
        at = shard * per + t
        tile = [
            jnp.where(shard == 1, b, a)
            for a, b in zip(*[frame.tile(s, t * BLOCK_ROWS) for s in (0, 1)])
        ]
        rows_of = (waves[0, pl.ds(2 * at, 2), :], waves[1, pl.ds(2 * at, 2), :])
        c, s = rope_tables(angles, tile[2], rows_of, 0, 1.0)
        live = jnp.where((row < tile[2]) | (row >= tile[3]), 1.0, 0.0).astype(jnp.bfloat16)
        into = pl.ds(pl.multiple_of(at * BLOCK_ROWS, BLOCK_ROWS), BLOCK_ROWS)
        of = pl.ds(pl.multiple_of(i * BLOCK_ROWS, BLOCK_ROWS), BLOCK_ROWS)
        lv[into, :] = live
        for h in range(kv_heads):
            cols = slice(h * HEAD_DIMENSION, (h + 1) * HEAD_DIMENSION)
            kr[h, into, :] = rotate(kb[of, cols], c, s)
            vz[h, into, :] = vb[of, cols] * live
        return carry

    lax.fori_loop(0, 2 * per, one, 0)


def visit_kernel(kind, step, shards, rows, index_ref, part_ref, spans, other, dirty, *refs):
    notes, refs = refs[: step // 2], refs[step // 2 :]
    if kind == "window":
        tail, refs = refs[0], refs[1:]
    angles, freq, kr, vz, lv, queries, out = refs[:7]
    scratch = refs[7:]
    index, part = index_ref[0], part_ref[0]
    odd = lax.rem(index, 2)
    held = dict(enumerate(chip_spans(index, rows, spans, other)))
    block = dirty[0]
    for chip, note in enumerate(notes, 1):
        note = read_note(note, 5)
        held[2 * chip], held[2 * chip + 1] = by_parity(odd, note[:2], note[2:4])
        block = note[4] - 1
    valid = (index + step < shards) & (block >= 0)
    out[...] = jnp.zeros(out.shape, out.dtype)

    @pl.when(valid)
    def _():
        edge = {"block": (step, step + 1)}
        if kind == "window":
            held[-1] = read_note(tail, 2)
            reach = (tail.shape[0] - NOTE_ROWS) // 2
            tail_tile = Frame(held, rows).tile(-1, rows - BLOCK_ROWS)
            edge["tail"] = tail.at[:reach, :], tail.at[reach : 2 * reach, :], tail_tile
        frame = Frame(held, rows)
        keys = (kr, vz, lv)
        visit(kind, index, block, frame, freq[...], angles, part, queries, keys, edge, out, scratch)


def last_kernel(rows, parts, spans, dirty, index_ref, *refs):
    out = refs[-1]
    index = index_ref[0]
    heads = out.shape[1] // HEAD_DIMENSION // parts
    width = heads * HEAD_DIMENSION
    block = dirty[0]
    first = index * rows + jnp.maximum(block, 0) * BLOCK_ROWS
    row = lax.broadcasted_iota(jnp.int32, (BLOCK_ROWS, LANES), 0) + first
    keep = ((row < spans[0, 0]) | (row >= spans[0, 1])) & (block >= 0)
    line = lax.broadcasted_iota(jnp.int32, (LANES, LANES), 0)

    def picker(head, of):
        return jnp.where((line == head) | (line == head + of), 1.0, 0.0).astype(jnp.bfloat16)

    own = refs[0]
    for part in range(parts):
        a, b = refs[1 + 2 * part : 3 + 2 * part]
        totals = jnp.concatenate([own[:, out.shape[1] :], a[:, width:], b[:, width:]], axis=1)
        for head in range(heads):
            pick = picker(head, heads)
            pick = jnp.concatenate([picker(part * heads + head, parts * heads), pick, pick], axis=0)
            total = jnp.dot(totals, pick, preferred_element_type=jnp.float32)
            total = jnp.where(total > 0, total, 1.0)
            cols = slice(head * HEAD_DIMENSION, (head + 1) * HEAD_DIMENSION)
            into = slice(part * width + cols.start, part * width + cols.stop)
            number = (
                own[:, into].astype(jnp.float32)
                + a[:, cols].astype(jnp.float32)
                + b[:, cols].astype(jnp.float32)
            )
            out[:, into] = jnp.where(keep, number / total, 0.0).astype(out.dtype)


SMEM = pl.BlockSpec(memory_space=pltpu.SMEM)
VMEM = pl.BlockSpec(memory_space=pltpu.VMEM)
HBM = pl.BlockSpec(memory_space=pltpu.HBM)


def in_hbm(array):
    return pltpu.with_memory_space_constraint(array, pltpu.HBM)


def work(queries, keys, values, dirty, spans):
    shards = lax.axis_size("seq")
    index = lax.axis_index("seq")
    rows, columns = keys.shape
    kv_heads = columns // HEAD_DIMENSION
    per = rows // BLOCK_ROWS
    back = WINDOW // rows
    reach = (back + 1) * SPAN
    swap = [(i, i ^ 1) for i in range(shards)]
    onward = [(i, i + 1) for i in range(1, shards - 1, 2)]

    parts = 2
    wide = queries.shape[1] // parts
    params = pltpu.CompilerParams(vmem_limit_bytes=VMEM_LIMIT)

    other = send(spans, swap)
    k_other = send(keys, swap)
    v_other = send(values, swap)
    *pieces, tail = pl.pallas_call(
        pack_kernel,
        out_shape=[
            jax.ShapeDtypeStruct((BLOCK_ROWS + (NOTE_ROWS if p == 0 else 0), wide), queries.dtype)
            for p in range(parts)
        ]
        + [jax.ShapeDtypeStruct((2 * reach + NOTE_ROWS, columns), keys.dtype)],
        in_specs=[SMEM] * 3 + [HBM] * 3,
        out_specs=[VMEM] * (parts + 1),
        scratch_shapes=[pltpu.SemaphoreType.DMA((parts + 2,))],
        compiler_params=params,
        cost_estimate=pl.CostEstimate(flops=1 << 20, bytes_accessed=4 << 20, transcendentals=0),
        name="pack",
    )(spans, other, dirty, in_hbm(keys), in_hbm(values), in_hbm(queries))
    near, far = [], []
    for piece in pieces:
        near.append(shift(piece, -back // 2))
        far.append(shift(piece, -back))
    tail = send(tail, onward)

    at = index.astype(jnp.int32).reshape(1)
    angles = jnp.asarray(row_angles())
    freq = jnp.asarray(lane_frequency()[None, :])
    part_heads = kv_heads // parts

    def payload(heads):
        return jax.ShapeDtypeStruct((BLOCK_ROWS, heads * HEAD_DIMENSION + LANES), jnp.bfloat16)

    by_head = pltpu.VMEM((kv_heads, 2 * rows, HEAD_DIMENSION), jnp.bfloat16)
    kr, vz, lv = pl.pallas_call(
        prepare_kernel,
        out_shape=(by_head, by_head, pltpu.VMEM((2 * rows, LANES), jnp.bfloat16)),
        in_specs=[SMEM] * 3 + [VMEM] * 2 + [HBM] * 4,
        out_specs=[VMEM] * 3,
        scratch_shapes=[
            pltpu.VMEM((2 * rows, columns), keys.dtype),
            pltpu.VMEM((2 * rows, columns), keys.dtype),
            pltpu.VMEM((2, -(-4 * per // 8) * 8, LANES), jnp.float32),
            pltpu.SemaphoreType.DMA((2, 2 * per)),
        ],
        compiler_params=params,
        cost_estimate=pl.CostEstimate(flops=1 << 24, bytes_accessed=20 << 20, transcendentals=0),
        name="prepare",
    )(at, spans, other, angles, freq, *map(in_hbm, (keys, k_other, values, v_other)))

    def visitor(kind, step, part, notes, query):
        count = {"own": per, "middle": 2 * per, "window": per}[kind] * BLOCK_ROWS
        heads = kv_heads if part is None else part_heads
        work = BLOCK_ROWS * 2 * heads * count
        edges = {"own": 1, "middle": 1, "window": 2}[kind]
        extra = [*notes, tail] if kind == "window" else notes
        return pl.pallas_call(
            functools.partial(visit_kernel, kind, step, shards, rows),
            out_shape=payload(2 * heads),
            in_specs=[SMEM] * 5 + [VMEM] * (6 + len(extra)),
            out_specs=VMEM,
            scratch_shapes=[
                pltpu.VMEM((BLOCK_ROWS, LANES), jnp.float32),
                pltpu.VMEM((2 * heads, BLOCK_ROWS, HEAD_DIMENSION), jnp.bfloat16),
                pltpu.VMEM((2 * heads, BLOCK_ROWS, HEAD_DIMENSION + LANES), jnp.float32),
                pltpu.VMEM((edges, heads, BLOCK_ROWS, HEAD_DIMENSION), jnp.bfloat16),
                pltpu.VMEM((edges, heads, BLOCK_ROWS, HEAD_DIMENSION), jnp.bfloat16),
                pltpu.VMEM((edges, BLOCK_ROWS, LANES), jnp.bfloat16),
            ],
            compiler_params=params,
            cost_estimate=pl.CostEstimate(
                flops=work * 4 * HEAD_DIMENSION, bytes_accessed=6 << 20, transcendentals=2 * work
            ),
        )(
            at, jnp.full((1,), part or 0, jnp.int32), spans, other, dirty,
            *extra, angles, freq, kr, vz, lv, query,
        )

    middle, window = [], []
    for p in range(parts):
        got = visitor("middle", back // 2, p, [near[0]], near[p])
        middle.append(shift(got, back // 2))
        got = visitor("window", back, p, [near[0], far[0]], far[p])
        window.append(shift(got, back))
    own = visitor("own", 0, None, [], queries)
    sums = [own] + [x for p in range(parts) for x in (middle[p], window[p])]
    return pl.pallas_call(
        functools.partial(last_kernel, rows, parts),
        out_shape=jax.ShapeDtypeStruct(queries.shape, queries.dtype),
        in_specs=[SMEM] * 3 + [VMEM] * len(sums),
        out_specs=VMEM,
        compiler_params=params,
        name="last",
    )(spans, dirty, at, *sums)


def solution(mesh):
    placed = (
        P(("groups", "seq"), None),
        P(("groups", "seq"), None),
        P(("groups", "seq"), None),
        P(("groups", "seq")),
        P(("groups", "seq"), None),
    )
    return jax.shard_map(
        work, mesh=mesh, in_specs=placed, out_specs=P(("groups", "seq"), None), check_vma=False
    )
```

time: 493 us -> 117 us (0.24)
  matrix products: 179 us -> 0 us
  waiting for transfers between devices: 194 us -> 65.4 us
  blocking collectives: 30 us -> 0 us
  Pallas kernels: 0 us -> 29 us
  other arithmetic: 26.7 us -> 0 us
  local copies, waits for them, and re-layouts: 20.1 us -> 1.98 us
  starting transfers between devices: 30.6 us -> 18.4 us
  between operations: 5.9 us -> 0.87 us
    dot_general x24 -> x0, matrix products: 179 us -> none  [the longest x12 91.1 us: visit(): jnp.einsum('nexi,inv->xnev', weight.astype(jnp.bfloat16), tile_v, preferr...]
    ppermute x15 -> x12, waiting for transfers between devices: 194 us -> 65.4 us  [send(): return lax.ppermute(array, 'seq', pairs)]
    pallas_call x0 -> x8, Pallas kernels: none -> 29 us  [the longest x5 18.6 us: visitor(): pl.pallas_call(functools.partial(visit_kernel, kind, step, shards, rows),...]
    all_gather x1 -> x0, blocking collectives: 16.9 us -> none  [body(): lax.all_gather(spans, 'seq', axis=0, tiled=True)]
    unnamed x1 -> x0, blocking collectives: 13.1 us -> none
    ppermute x15 -> x12, starting transfers between devices: 30.6 us -> 18.4 us  [send(): return lax.ppermute(array, 'seq', pairs)]
    unnamed x17 -> x12, local copies, waits for them, and re-layouts: 11.2 us -> 1.98 us
    convert_element_type x4 -> x0, other arithmetic: 8.12 us -> none  [the longest x1 5.98 us: body(): result.reshape(BLOCK_ROWS, q_heads * HEAD_DIMENSION).astype(jnp.bfloat16)]
  transfers between devices with their start and end apart: 15 -> 12, of which waited for: 4 -> 6; matrix products, arithmetic and copies ran while one was open for 43% -> 0% of each run, Pallas kernels for 0% -> 23%
where the time goes in v1:
time: 117 us; the launch traced here: 116 us
  waiting for transfers between devices  65.4 us (56%)
  Pallas kernels  29 us (25%)
  starting transfers between devices  18.4 us (16%)
  local copies, waits for them, and re-layouts  1.98 us (2%)
    ppermute x12, waiting for transfers between devices, send(): return lax.ppermute(array, 'seq', pairs)  65.4 us
    pallas_call x5, Pallas kernels, visitor(): pl.pallas_call(functools.partial(visit_kernel, kind, step, shards, rows),...  18.6 us
    ppermute x12, starting transfers between devices, send(): return lax.ppermute(array, 'seq', pairs)  18.4 us
    pallas_call x1, Pallas kernels, work(): pl.pallas_call(prepare_kernel, out_shape=(by_head, by_head, pltpu.VMEM((2...  4.95 us
    pallas_call x1, Pallas kernels, work(): pl.pallas_call(pack_kernel, out_shape=[jax.ShapeDtypeStruct((BLOCK_ROWS +...  2.93 us
    pallas_call x1, Pallas kernels, work(): pl.pallas_call(functools.partial(last_kernel, rows, parts), out_shape=jax...  2.57 us
  transfers between devices with their start and end apart: 12, of which 6 were waited for; matrix products, arithmetic and copies ran while one was open for 0% of the time, Pallas kernels for 23%

profile of v1, /device:TPU:28, one launch (start us, length us, event | category | flops | bytes accessed | tf_op | source)
XLA Modules:
  0.0 115.7 jit_solution(4400137376742838206)
XLA Ops:
  1.2 6.3 %collective-permute-done.other = s32[1,2]{1,0:T(1,128)S(1)} collective-permute-done((s32[1,2]{1,0:T(1,128)}, s32[1,2]{1,0:T(1,128)S(1)}, u32[]{:S(2)}, u32[]{:S(2)}) %collective-permute-start) | collective-permute-done | bytes 40 | tf_op jit(solution)/shard_map/ppermute | solution.py:42
  8.2 2.9 %pack.1 = (bf16[264,1024]{1,0:T(8,128)(2,1)}, bf16[256,1024]{1,0:T(8,128)(2,1)}, bf16[328,1024]{1,0:T(8,128)(2,1)S(1)}) custom-call(s32[1,2]{1,0:T(1,128)S(1)} %copy-done.2, s32[1,2]{1,0:T(1,128)S(1)} %collective-permute-done.other, s32[1]{0:T(128)S(6)} %copy.8.dirty, bf16[1024,1024]{1,0:T(8,128)(2,1)} %keys.1, bf16[1024,1024]{1,0:T(8,128)(2,1)} %values.1, ...), custom_call_target="tpu_custom_call" | custom-call | flops 1048576 | bytes 4194304 | tf_op jit(solution)/shard_map/pack/pallas_call | solution.py:422
  11.1 1.3 %collective-permute-start.6 = (bf16[328,1024]{1,0:T(8,128)(2,1)S(1)}, bf16[328,1024]{1,0:T(8,128)(2,1)S(1)}, u32[]{:S(2)}, u32[]{:S(2)}) collective-permute-start(bf16[328,1024]{1,0:T(8,128)(2,1)S(1)} %get-tuple-element.15), channel_id=1, source_target_pairs={{1,2},{3,4},{5,6},{7,8},{9,10},{11,12},{13,14},{17,18},{19,20},{21... | collective-permute-start | bytes 2015240 | tf_op jit(solution)/shard_map/ppermute | solution.py:42
  12.4 3.3 %collective-permute-start.3 = (bf16[264,1024]{1,0:T(8,128)(2,1)}, bf16[264,1024]{1,0:T(8,128)(2,1)S(1)}, u32[]{:S(2)}, u32[]{:S(2)}) collective-permute-start(bf16[264,1024]{1,0:T(8,128)(2,1)} %get-tuple-element.14), channel_id=1, source_target_pairs={{2,0},{3,1},{4,2},{5,3},{6,4},{7,5},{8,6},{9,7},{10,8},{11,9},{12,... | collective-permute-start | bytes 1622024 | tf_op jit(solution)/shard_map/ppermute | solution.py:42
  15.7 2.4 %collective-permute-start.5 = (bf16[264,1024]{1,0:T(8,128)(2,1)}, bf16[264,1024]{1,0:T(8,128)(2,1)S(1)}, u32[]{:S(2)}, u32[]{:S(2)}) collective-permute-start(bf16[264,1024]{1,0:T(8,128)(2,1)} %get-tuple-element.14), channel_id=1, source_target_pairs={{4,0},{5,1},{6,2},{7,3},{8,4},{9,5},{10,6},{11,7},{12,8},{13,9},{1... | collective-permute-start | bytes 1622024 | tf_op jit(solution)/shard_map/ppermute | solution.py:42
  18.1 1.3 %copy-done.5 = bf16[1024,1024]{1,0:T(8,128)(2,1)} copy-done((bf16[1024,1024]{1,0:T(8,128)(2,1)}, bf16[1024,1024]{1,0:T(8,128)(2,1)S(1)}, u32[]{:S(2)}) %copy-start.5) | copy-done | bytes 2097176
  19.4 2.3 %collective-permute-start.10 = (bf16[256,1024]{1,0:T(8,128)(2,1)}, bf16[256,1024]{1,0:T(8,128)(2,1)S(1)}, u32[]{:S(2)}, u32[]{:S(2)}) collective-permute-start(bf16[256,1024]{1,0:T(8,128)(2,1)} %get-tuple-element.16), channel_id=1, source_target_pairs={{4,0},{5,1},{6,2},{7,3},{8,4},{9,5},{10,6},{11,7},{12,8},{13,9},{1... | collective-permute-start | bytes 1572872 | tf_op jit(solution)/shard_map/ppermute | solution.py:42
  21.8 2.0 %collective-permute-start.8 = (bf16[256,1024]{1,0:T(8,128)(2,1)}, bf16[256,1024]{1,0:T(8,128)(2,1)}, u32[]{:S(2)}, u32[]{:S(2)}) collective-permute-start(bf16[256,1024]{1,0:T(8,128)(2,1)} %get-tuple-element.16), channel_id=1, source_target_pairs={{2,0},{3,1},{4,2},{5,3},{6,4},{7,5},{8,6},{9,7},{10,8},{11,9},{12,... | collective-permute-start | bytes 1572872 | tf_op jit(solution)/shard_map/ppermute | solution.py:42
  23.8 5.0 %prepare.1 = (bf16[8,2048,128]{2,1,0:T(8,128)(2,1)S(1)}, bf16[8,2048,128]{2,1,0:T(8,128)(2,1)S(1)}, bf16[2048,128]{1,0:T(8,128)(2,1)S(1)}) custom-call(s32[1]{0:T(128)} %bitcast.index_ref, s32[1,2]{1,0:T(1,128)S(1)} %copy-done.3, s32[1,2]{1,0:T(1,128)S(1)} %collective-permute-done.other, f32[2,256,128]{2,1,0:T(8,128)S(1)} %copy-done, ...), custom_call_target="tpu_custom_call" | custom-call | flops 16777216 | bytes 20971520 | tf_op jit(solution)/shard_map/prepare/pallas_call | solution.py:451
  28.8 21.5 %collective-permute-done.10.refs_8_ = bf16[256,1024]{1,0:T(8,128)(2,1)S(1)} collective-permute-done((bf16[256,1024]{1,0:T(8,128)(2,1)}, bf16[256,1024]{1,0:T(8,128)(2,1)S(1)}, u32[]{:S(2)}, u32[]{:S(2)}) %collective-permute-start.10) | collective-permute-done | bytes 524320 | tf_op jit(solution)/shard_map/ppermute | solution.py:42
  50.2 0.7 shard_map.77
  50.9 1.3 %collective-permute-start.11 = (bf16[256,1152]{1,0:T(8,128)(2,1)S(1)}, bf16[256,1152]{1,0:T(8,128)(2,1)S(1)}, u32[]{:S(2)}, u32[]{:S(2)}) collective-permute-start(bf16[256,1152]{1,0:T(8,128)(2,1)S(1)} %shard_map.77), channel_id=1, source_target_pairs={{0,4},{1,5},{2,6},{3,7},{4,8},{5,9},{6,10},{7,11},{8,12},{9,13},{1... | collective-permute-start | bytes 1769480 | tf_op jit(solution)/shard_map/ppermute | solution.py:42
  52.2 9.2 %collective-permute-done.8.refs_6_ = bf16[256,1024]{1,0:T(8,128)(2,1)} collective-permute-done((bf16[256,1024]{1,0:T(8,128)(2,1)}, bf16[256,1024]{1,0:T(8,128)(2,1)}, u32[]{:S(2)}, u32[]{:S(2)}) %collective-permute-start.8) | collective-permute-done | bytes 524320 | tf_op jit(solution)/shard_map/ppermute | solution.py:42
  61.5 7.3 %shard_map.76 = bf16[256,1152]{1,0:T(8,128)(2,1)S(1)} custom-call(s32[1]{0:T(128)} %bitcast.index_ref, s32[1]{0:T(128)} %constant.4.clone.1.part_ref, s32[1,2]{1,0:T(1,128)S(1)} %copy-done.3, s32[1,2]{1,0:T(1,128)S(1)} %collective-permute-done.other, s32[1]{0:T(128)S(6)} %copy.8.dirty, bf16[264,1024]{1,0:T(8,128)(2,1)S(1)} %collective-permute-done.3.refs_0_.refs_6_, ...), custom_call_target="tpu_custom_call" | custom-call | flops 2147483648 | bytes 6291456 | tf_op jit(solution)/shard_map/pallas_call | solution.py:473
  68.8 1.9 %collective-permute-start.9 = (bf16[256,1152]{1,0:T(8,128)(2,1)S(1)}, bf16[256,1152]{1,0:T(8,128)(2,1)S(1)}, u32[]{:S(2)}, u32[]{:S(2)}) collective-permute-start(bf16[256,1152]{1,0:T(8,128)(2,1)S(1)} %shard_map.76), channel_id=1, source_target_pairs={{0,2},{1,3},{2,4},{3,5},{4,6},{5,7},{6,8},{7,9},{8,10},{9,11},{10,... | collective-permute-start | bytes 1769480 | tf_op jit(solution)/shard_map/ppermute | solution.py:42
  70.7 0.7 shard_map.75
  71.4 1.4 %collective-permute-start.7 = (bf16[256,1152]{1,0:T(8,128)(2,1)S(1)}, bf16[256,1152]{1,0:T(8,128)(2,1)S(1)}, u32[]{:S(2)}, u32[]{:S(2)}) collective-permute-start(bf16[256,1152]{1,0:T(8,128)(2,1)S(1)} %shard_map.75), channel_id=1, source_target_pairs={{0,4},{1,5},{2,6},{3,7},{4,8},{5,9},{6,10},{7,11},{8,12},{9,13},{1... | collective-permute-start | bytes 1769480 | tf_op jit(solution)/shard_map/ppermute | solution.py:42
  72.9 7.0 %shard_map.74 = bf16[256,1152]{1,0:T(8,128)(2,1)S(1)} custom-call(s32[1]{0:T(128)} %bitcast.index_ref, s32[1]{0:T(128)} %constant.3.clone.1.part_ref, s32[1,2]{1,0:T(1,128)S(1)} %copy-done.3, s32[1,2]{1,0:T(1,128)S(1)} %collective-permute-done.other, s32[1]{0:T(128)S(6)} %copy.8.dirty, bf16[264,1024]{1,0:T(8,128)(2,1)S(1)} %collective-permute-done.3.refs_0_.refs_6_, ...), custom_call_target="tpu_custom_call" | custom-call | flops 2147483648 | bytes 6291456 | tf_op jit(solution)/shard_map/pallas_call | solution.py:473
  79.9 1.9 %collective-permute-start.4 = (bf16[256,1152]{1,0:T(8,128)(2,1)S(1)}, bf16[256,1152]{1,0:T(8,128)(2,1)S(1)}, u32[]{:S(2)}, u32[]{:S(2)}) collective-permute-start(bf16[256,1152]{1,0:T(8,128)(2,1)S(1)} %shard_map.74), channel_id=1, source_target_pairs={{0,2},{1,3},{2,4},{3,5},{4,6},{5,7},{6,8},{7,9},{8,10},{9,11},{10,... | collective-permute-start | bytes 1769480 | tf_op jit(solution)/shard_map/ppermute | solution.py:42
  81.8 2.8 %shard_map.73.refs_0_ = bf16[256,2176]{1,0:T(8,128)(2,1)S(1)} custom-call(s32[1]{0:T(128)} %bitcast.index_ref, s32[1]{0:T(128)} %constant.3.clone.1.part_ref, s32[1,2]{1,0:T(1,128)S(1)} %copy-done.3, s32[1,2]{1,0:T(1,128)S(1)} %collective-permute-done.other, s32[1]{0:T(128)S(6)} %copy.8.dirty, f32[2,256,128]{2,1,0:T(8,128)S(1)} %copy-done, ...), custom_call_target="tpu_custom_call" | custom-call | flops 2147483648 | bytes 6291456 | tf_op jit(solution)/shard_map/pallas_call | solution.py:473
  84.7 3.1 %collective-permute-done.9.refs_3_ = bf16[256,1152]{1,0:T(8,128)(2,1)S(1)} collective-permute-done((bf16[256,1152]{1,0:T(8,128)(2,1)S(1)}, bf16[256,1152]{1,0:T(8,128)(2,1)S(1)}, u32[]{:S(2)}, u32[]{:S(2)}) %collective-permute-start.9) | collective-permute-done | bytes 589856 | tf_op jit(solution)/shard_map/ppermute | solution.py:42
  87.8 7.7 %collective-permute-done.7.refs_2_ = bf16[256,1152]{1,0:T(8,128)(2,1)S(1)} collective-permute-done((bf16[256,1152]{1,0:T(8,128)(2,1)S(1)}, bf16[256,1152]{1,0:T(8,128)(2,1)S(1)}, u32[]{:S(2)}, u32[]{:S(2)}) %collective-permute-start.7) | collective-permute-done | bytes 589856 | tf_op jit(solution)/shard_map/ppermute | solution.py:42
  95.5 17.6 %collective-permute-done.4.refs_1_ = bf16[256,1152]{1,0:T(8,128)(2,1)S(1)} collective-permute-done((bf16[256,1152]{1,0:T(8,128)(2,1)S(1)}, bf16[256,1152]{1,0:T(8,128)(2,1)S(1)}, u32[]{:S(2)}, u32[]{:S(2)}) %collective-permute-start.4) | collective-permute-done | bytes 589856 | tf_op jit(solution)/shard_map/ppermute | solution.py:42
  113.1 2.6 %last.1 = bf16[256,2048]{1,0:T(8,128)(2,1)} custom-call(s32[1,2]{1,0:T(1,128)S(1)} %copy-done.3, s32[1]{0:T(128)S(6)} %copy.8.dirty, s32[1]{0:T(128)} %bitcast.index_ref, bf16[256,2176]{1,0:T(8,128)(2,1)S(1)} %shard_map.73.refs_0_, bf16[256,1152]{1,0:T(8,128)(2,1)S(1)} %collective-permute-done.4.refs_1_, ...), custom_call_target="tpu_custom_call" | custom-call | tf_op jit(solution)/shard_map/last/pallas_call | solution.py:503
  (20 shorter events, 1.2 us)
Async XLA Ops:
  0.0 18.1 %collective-permute-start.1 = (bf16[1024,1024]{1,0:T(8,128)(2,1)}, bf16[1024,1024]{1,0:T(8,128)(2,1)S(1)}, u32[]{:S(2)}, u32[]{:S(2)}) collective-permute-start(bf16[1024,1024]{1,0:T(8,128)(2,1)} %keys.1), channel_id=1, source_target_pairs={{0,1},{1,0},{2,3},{3,2},{4,5},{5,4},{6,7},{7,6},{8,9},{9,8},{10,11... | collective-permute-start | bytes 6291464 | tf_op jit(solution)/shard_map/ppermute | solution.py:42
  0.0 21.8 %collective-permute-start.2 = (bf16[1024,1024]{1,0:T(8,128)(2,1)}, bf16[1024,1024]{1,0:T(8,128)(2,1)}, u32[]{:S(2)}, u32[]{:S(2)}) collective-permute-start(bf16[1024,1024]{1,0:T(8,128)(2,1)} %values.1), channel_id=1, source_target_pairs={{0,1},{1,0},{2,3},{3,2},{4,5},{5,4},{6,7},{7,6},{8,9},{9,8},{10,11... | collective-permute-start | bytes 6291464 | tf_op jit(solution)/shard_map/ppermute | solution.py:42
  0.5 7.0 %collective-permute-start = (s32[1,2]{1,0:T(1,128)}, s32[1,2]{1,0:T(1,128)S(1)}, u32[]{:S(2)}, u32[]{:S(2)}) collective-permute-start(s32[1,2]{1,0:T(1,128)} %spans.15), channel_id=1, source_target_pairs={{0,1},{1,0},{2,3},{3,2},{4,5},{5,4},{6,7},{7,6},{8,9},{9,8},{10,11... | collective-permute-start | bytes 32 | tf_op jit(solution)/shard_map/ppermute | solution.py:42
  1.2 22.6 %copy-start = (f32[2,256,128]{2,1,0:T(8,128)S(1)}, f32[2,256,128]{2,1,0:T(8,128)}, u32[]{:S(2)}) copy-start(f32[2,256,128]{2,1,0:T(8,128)} %constant.12.clone.angles.refs_0_.refs_1_.refs_3_) | copy-start | bytes 786436
  7.5 0.7 copy-start.2
  8.2 15.6 %copy-start.3 = (s32[1,2]{1,0:T(1,128)S(1)}, s32[1,2]{1,0:T(1,128)}, u32[]{:S(2)}) copy-start(s32[1,2]{1,0:T(1,128)} %spans.15) | copy-start | bytes 28
  8.2 15.6 %copy-start.4 = (f32[1,128]{1,0:T(1,128)S(1)}, f32[1,128]{1,0:T(1,128)}, u32[]{:S(2)}) copy-start(f32[1,128]{1,0:T(1,128)} %constant.13.clone.freq.refs_1_.refs_2_.refs_4_) | copy-start | bytes 1540
  11.1 39.1 %collective-permute-start.6 = (bf16[328,1024]{1,0:T(8,128)(2,1)S(1)}, bf16[328,1024]{1,0:T(8,128)(2,1)S(1)}, u32[]{:S(2)}, u32[]{:S(2)}) collective-permute-start(bf16[328,1024]{1,0:T(8,128)(2,1)S(1)} %get-tuple-element.15), channel_id=1, source_target_pairs={{1,2},{3,4},{5,6},{7,8},{9,10},{11,12},{13,14},{17,18},{19,20},{21... | collective-permute-start | bytes 2015240 | tf_op jit(solution)/shard_map/ppermute | solution.py:42
  12.4 37.8 %collective-permute-start.3 = (bf16[264,1024]{1,0:T(8,128)(2,1)}, bf16[264,1024]{1,0:T(8,128)(2,1)S(1)}, u32[]{:S(2)}, u32[]{:S(2)}) collective-permute-start(bf16[264,1024]{1,0:T(8,128)(2,1)} %get-tuple-element.14), channel_id=1, source_target_pairs={{2,0},{3,1},{4,2},{5,3},{6,4},{7,5},{8,6},{9,7},{10,8},{11,9},{12,... | collective-permute-start | bytes 1622024 | tf_op jit(solution)/shard_map/ppermute | solution.py:42
  15.7 34.5 %collective-permute-start.5 = (bf16[264,1024]{1,0:T(8,128)(2,1)}, bf16[264,1024]{1,0:T(8,128)(2,1)S(1)}, u32[]{:S(2)}, u32[]{:S(2)}) collective-permute-start(bf16[264,1024]{1,0:T(8,128)(2,1)} %get-tuple-element.14), channel_id=1, source_target_pairs={{4,0},{5,1},{6,2},{7,3},{8,4},{9,5},{10,6},{11,7},{12,8},{13,9},{1... | collective-permute-start | bytes 1622024 | tf_op jit(solution)/shard_map/ppermute | solution.py:42
  18.1 1.3 %copy-start.5 = (bf16[1024,1024]{1,0:T(8,128)(2,1)}, bf16[1024,1024]{1,0:T(8,128)(2,1)S(1)}, u32[]{:S(2)}) copy-start(bf16[1024,1024]{1,0:T(8,128)(2,1)S(1)} %collective-permute-done.1.k_other) | copy-start | bytes 6291460
  19.4 30.8 %collective-permute-start.10 = (bf16[256,1024]{1,0:T(8,128)(2,1)}, bf16[256,1024]{1,0:T(8,128)(2,1)S(1)}, u32[]{:S(2)}, u32[]{:S(2)}) collective-permute-start(bf16[256,1024]{1,0:T(8,128)(2,1)} %get-tuple-element.16), channel_id=1, source_target_pairs={{4,0},{5,1},{6,2},{7,3},{8,4},{9,5},{10,6},{11,7},{12,8},{13,9},{1... | collective-permute-start | bytes 1572872 | tf_op jit(solution)/shard_map/ppermute | solution.py:42
  21.8 39.7 %collective-permute-start.8 = (bf16[256,1024]{1,0:T(8,128)(2,1)}, bf16[256,1024]{1,0:T(8,128)(2,1)}, u32[]{:S(2)}, u32[]{:S(2)}) collective-permute-start(bf16[256,1024]{1,0:T(8,128)(2,1)} %get-tuple-element.16), channel_id=1, source_target_pairs={{2,0},{3,1},{4,2},{5,3},{6,4},{7,5},{8,6},{9,7},{10,8},{11,9},{12,... | collective-permute-start | bytes 1572872 | tf_op jit(solution)/shard_map/ppermute | solution.py:42
  50.9 33.7 %collective-permute-start.11 = (bf16[256,1152]{1,0:T(8,128)(2,1)S(1)}, bf16[256,1152]{1,0:T(8,128)(2,1)S(1)}, u32[]{:S(2)}, u32[]{:S(2)}) collective-permute-start(bf16[256,1152]{1,0:T(8,128)(2,1)S(1)} %shard_map.77), channel_id=1, source_target_pairs={{0,4},{1,5},{2,6},{3,7},{4,8},{5,9},{6,10},{7,11},{8,12},{9,13},{1... | collective-permute-start | bytes 1769480 | tf_op jit(solution)/shard_map/ppermute | solution.py:42
  68.8 19.0 %collective-permute-start.9 = (bf16[256,1152]{1,0:T(8,128)(2,1)S(1)}, bf16[256,1152]{1,0:T(8,128)(2,1)S(1)}, u32[]{:S(2)}, u32[]{:S(2)}) collective-permute-start(bf16[256,1152]{1,0:T(8,128)(2,1)S(1)} %shard_map.76), channel_id=1, source_target_pairs={{0,2},{1,3},{2,4},{3,5},{4,6},{5,7},{6,8},{7,9},{8,10},{9,11},{10,... | collective-permute-start | bytes 1769480 | tf_op jit(solution)/shard_map/ppermute | solution.py:42
  71.4 10.4 %copy-start.1 = (bf16[256,2048]{1,0:T(8,128)(2,1)S(1)}, bf16[256,2048]{1,0:T(8,128)(2,1)}, u32[]{:S(2)}) copy-start(bf16[256,2048]{1,0:T(8,128)(2,1)} %query.1) | copy-start | bytes 3145732
  71.4 24.1 %collective-permute-start.7 = (bf16[256,1152]{1,0:T(8,128)(2,1)S(1)}, bf16[256,1152]{1,0:T(8,128)(2,1)S(1)}, u32[]{:S(2)}, u32[]{:S(2)}) collective-permute-start(bf16[256,1152]{1,0:T(8,128)(2,1)S(1)} %shard_map.75), channel_id=1, source_target_pairs={{0,4},{1,5},{2,6},{3,7},{4,8},{5,9},{6,10},{7,11},{8,12},{9,13},{1... | collective-permute-start | bytes 1769480 | tf_op jit(solution)/shard_map/ppermute | solution.py:42
  79.9 33.2 %collective-permute-start.4 = (bf16[256,1152]{1,0:T(8,128)(2,1)S(1)}, bf16[256,1152]{1,0:T(8,128)(2,1)S(1)}, u32[]{:S(2)}, u32[]{:S(2)}) collective-permute-start(bf16[256,1152]{1,0:T(8,128)(2,1)S(1)} %shard_map.74), channel_id=1, source_target_pairs={{0,2},{1,3},{2,4},{3,5},{4,6},{5,7},{6,8},{7,9},{8,10},{9,11},{10,... | collective-permute-start | bytes 1769480 | tf_op jit(solution)/shard_map/ppermute | solution.py:42

commit v2 on v1

--- a/solution.py
+++ b/solution.py
@@ -23,6 +23,7 @@
 HALF = HEAD_DIMENSION // 2
 LANES = 128
 NOTE_ROWS = 8
+SECOND_PART = 3
 DIGIT = 32
 VMEM_LIMIT = 32 << 20
 
@@ -80,8 +81,8 @@
     ref[ref.shape[0] - NOTE_ROWS :, :] = row.astype(jnp.float32).astype(jnp.bfloat16)
 
 
-def read_note(ref, count):
-    low = ref[ref.shape[0] - NOTE_ROWS :, :LANES].astype(jnp.float32)
+def read_note(note, count):
+    low = note.astype(jnp.float32)
     shape = (NOTE_ROWS, LANES)
     lane = lax.broadcasted_iota(jnp.int32, shape, 1)
     first = lax.broadcasted_iota(jnp.int32, shape, 0) == 0
@@ -125,21 +126,20 @@
     return row + jnp.where(row < begin, first, later)
 
 
-def visit(kind, index, block, frame, freq, angles, part, query, keys, edge, out, scratch):
+def visit(kind, index, block, frame, freq, angles, low, query, keys, edge, out, scratch):
     kr, vz, lv = keys
-    _, rot, acc, ke, ve, le = scratch
+    rot, acc, ke, ve, le = scratch
     odd = lax.rem(index, 2)
     per = frame.rows // BLOCK_ROWS
     q_heads = acc.shape[0]
     kv_heads = q_heads // 2
-    low = part * kv_heads
     pair = [frame.tile(s, block * BLOCK_ROWS) for s in edge["block"]]
     tile = [jnp.where(odd == 1, b, a) for a, b in zip(*pair)]
     waves = wave([tile[0], tile[1]], freq)
     c, s = rope_tables(angles, tile[2], waves, 0, QUERY_SCALE)
     for head in range(q_heads):
         cols = slice(head * HEAD_DIMENSION, (head + 1) * HEAD_DIMENSION)
-        rot[head] = rotate(query[:BLOCK_ROWS, cols], c, s)
+        rot[head] = rotate(query(cols), c, s)
     own = places(tile, 0, (BLOCK_ROWS, 1))
 
     def add(head, keys_of, values_of, keep, fresh):
@@ -219,8 +219,7 @@
             le[0] = jnp.where(live, 1.0, 0.0).astype(jnp.bfloat16)
             zero = jnp.zeros((BLOCK_ROWS - reach, HEAD_DIMENSION), jnp.bfloat16)
             for i in range(kv_heads):
-                at = pl.multiple_of((low + i) * HEAD_DIMENSION, HEAD_DIMENSION)
-                cols = pl.ds(at, HEAD_DIMENSION)
+                cols = slice((low + i) * HEAD_DIMENSION, (low + i + 1) * HEAD_DIMENSION)
                 ke[0, i] = rotate(jnp.concatenate([zero, tail_k[:, cols]], axis=0), c, s)
                 ve[0, i] = jnp.concatenate([zero, tail_v[:, cols]], axis=0) * le[0]
 
@@ -240,23 +239,27 @@
     sums = jnp.zeros((BLOCK_ROWS, LANES), jnp.float32)
     for head in range(q_heads):
         cols = slice(head * HEAD_DIMENSION, (head + 1) * HEAD_DIMENSION)
-        out[:, cols] = acc[head, :, :HEAD_DIMENSION].astype(jnp.bfloat16)
+        out[:BLOCK_ROWS, cols] = acc[head, :, :HEAD_DIMENSION].astype(jnp.bfloat16)
         t = acc[head, :, HEAD_DIMENSION:]
         high = t.astype(jnp.bfloat16).astype(jnp.float32)
         sums = jnp.where(lane == head, high, jnp.where(lane == head + q_heads, t - high, sums))
-    out[:, q_heads * HEAD_DIMENSION :] = sums.astype(jnp.bfloat16)
-
-
-def pack_kernel(spans, other, dirty, keys, values, query, *refs):
-    parts = refs[:-2]
-    tail, sem = refs[-2:]
+    sums = jnp.transpose(sums).astype(jnp.bfloat16)
+    groups = [sums[k * NOTE_ROWS : (k + 1) * NOTE_ROWS] for k in range(-(-2 * q_heads // NOTE_ROWS))]
+    rest = out.shape[1] - len(groups) * BLOCK_ROWS
+    out[BLOCK_ROWS:, :] = jnp.concatenate(groups + [jnp.zeros((NOTE_ROWS, rest), jnp.bfloat16)], axis=1)
+
+
+def cut_kernel(query, piece, sem):
+    copy = pltpu.make_async_copy(query.at[:, : piece.shape[1]], piece, sem)
+    copy.start()
+    copy.wait()
+
+
+def pack_kernel(spans, other, dirty, keys, values, query, piece, tail, note, sem):
     rows = keys.shape[0]
-    width = parts[0].shape[1]
     reach = (tail.shape[0] - NOTE_ROWS) // 2
     copies = [
-        (query.at[:, p * width : (p + 1) * width], part.at[:BLOCK_ROWS]) for p, part in enumerate(parts)
-    ]
-    copies += [
+        (query.at[:, query.shape[1] - piece.shape[1] :], piece),
         (keys.at[rows - reach :], tail.at[:reach]),
         (values.at[rows - reach :], tail.at[reach : 2 * reach]),
     ]
@@ -264,10 +267,12 @@
     for copy in copies:
         copy.start()
     mine = [lax.rem(spans[0, 0], rows), spans[0, 1] - spans[0, 0]]
-    write_note(
-        parts[0], mine + [lax.rem(other[0, 0], rows), other[0, 1] - other[0, 0], dirty[0] + 1]
-    )
     write_note(tail, mine)
+    others = [lax.rem(other[0, 0], rows), other[0, 1] - other[0, 0]]
+    for k, number in enumerate(mine + others + [dirty[0] + 1]):
+        note[k] = number
+    for k in range(5, note.shape[0]):
+        note[k] = 0
     for copy in copies:
         copy.wait()
 
@@ -329,67 +334,85 @@
     lax.fori_loop(0, 2 * per, one, 0)
 
 
-def visit_kernel(kind, step, shards, rows, index_ref, part_ref, spans, other, dirty, *refs):
-    notes, refs = refs[: step // 2], refs[step // 2 :]
-    if kind == "window":
-        tail, refs = refs[0], refs[1:]
-    angles, freq, kr, vz, lv, queries, out = refs[:7]
-    scratch = refs[7:]
-    index, part = index_ref[0], part_ref[0]
+def visit_kernel(kind, step, shards, rows, low, index_ref, spans, other, dirty, *refs):
+    index = index_ref[0]
     odd = lax.rem(index, 2)
     held = dict(enumerate(chip_spans(index, rows, spans, other)))
     block = dirty[0]
-    for chip, note in enumerate(notes, 1):
-        note = read_note(note, 5)
-        held[2 * chip], held[2 * chip + 1] = by_parity(odd, note[:2], note[2:4])
+    through = lax.rem(index // 2, 2) == 1
+    if kind == "window":
+        near_note, note, tail, *refs = refs
+        held[2] = (0, near_note[1] + near_note[3])
+        held[3] = (0, 0)
+    elif kind == "middle":
+        note, direct, relayed, *refs = refs
+    if kind != "own":
+        held[step], held[step + 1] = by_parity(odd, (note[0], note[1]), (note[2], note[3]))
         block = note[4] - 1
+    angles, freq, kr, vz, lv, *refs = refs
+    if kind == "middle":
+
+        def query(cols):
+            a = direct[:BLOCK_ROWS, cols].astype(jnp.float32)
+            return jnp.where(through, relayed[:BLOCK_ROWS, cols].astype(jnp.float32), a)
+    else:
+        queries, *refs = refs
+        query = lambda cols: queries[:BLOCK_ROWS, cols]
+    out, *scratch = refs
     valid = (index + step < shards) & (block >= 0)
-    out[...] = jnp.zeros(out.shape, out.dtype)
+
+    @pl.when(jnp.logical_not(valid))
+    def _():
+        out[...] = jnp.zeros(out.shape, out.dtype)
 
     @pl.when(valid)
     def _():
         edge = {"block": (step, step + 1)}
         if kind == "window":
-            held[-1] = read_note(tail, 2)
+            held[-1] = read_note(tail[tail.shape[0] - NOTE_ROWS :, :LANES], 2)
             reach = (tail.shape[0] - NOTE_ROWS) // 2
             tail_tile = Frame(held, rows).tile(-1, rows - BLOCK_ROWS)
             edge["tail"] = tail.at[:reach, :], tail.at[reach : 2 * reach, :], tail_tile
         frame = Frame(held, rows)
         keys = (kr, vz, lv)
-        visit(kind, index, block, frame, freq[...], angles, part, queries, keys, edge, out, scratch)
-
-
-def last_kernel(rows, parts, spans, dirty, index_ref, *refs):
-    out = refs[-1]
+        visit(kind, index, block, frame, freq[...], angles, low, query, keys, edge, out, scratch)
+
+
+def last_kernel(rows, low, spans, dirty, index_ref, own, a, b, *refs):
+    out, result, sem = refs[-3:]
     index = index_ref[0]
-    heads = out.shape[1] // HEAD_DIMENSION // parts
-    width = heads * HEAD_DIMENSION
+    heads = result.shape[1] // HEAD_DIMENSION
     block = dirty[0]
     first = index * rows + jnp.maximum(block, 0) * BLOCK_ROWS
     row = lax.broadcasted_iota(jnp.int32, (BLOCK_ROWS, LANES), 0) + first
     keep = ((row < spans[0, 0]) | (row >= spans[0, 1])) & (block >= 0)
+    rows_of, heads_of = [], []
+    for ref, count, lowest in ((own, own.shape[1] // HEAD_DIMENSION, 0), (a, heads, low), (b, heads, low)):
+        for k in range(-(-2 * count // NOTE_ROWS)):
+            rows_of.append(ref[BLOCK_ROWS:, k * BLOCK_ROWS : (k + 1) * BLOCK_ROWS].astype(jnp.float32))
+            for r in range(k * NOTE_ROWS, (k + 1) * NOTE_ROWS):
+                heads_of.append(lowest + r % count if r < 2 * count else -1)
+    rows_of.append(jnp.zeros((LANES - len(heads_of), BLOCK_ROWS), jnp.float32))
+    totals = jnp.transpose(jnp.concatenate(rows_of, axis=0)).astype(jnp.bfloat16)
     line = lax.broadcasted_iota(jnp.int32, (LANES, LANES), 0)
-
-    def picker(head, of):
-        return jnp.where((line == head) | (line == head + of), 1.0, 0.0).astype(jnp.bfloat16)
-
-    own = refs[0]
-    for part in range(parts):
-        a, b = refs[1 + 2 * part : 3 + 2 * part]
-        totals = jnp.concatenate([own[:, out.shape[1] :], a[:, width:], b[:, width:]], axis=1)
-        for head in range(heads):
-            pick = picker(head, heads)
-            pick = jnp.concatenate([picker(part * heads + head, parts * heads), pick, pick], axis=0)
-            total = jnp.dot(totals, pick, preferred_element_type=jnp.float32)
-            total = jnp.where(total > 0, total, 1.0)
-            cols = slice(head * HEAD_DIMENSION, (head + 1) * HEAD_DIMENSION)
-            into = slice(part * width + cols.start, part * width + cols.stop)
-            number = (
-                own[:, into].astype(jnp.float32)
-                + a[:, cols].astype(jnp.float32)
-                + b[:, cols].astype(jnp.float32)
-            )
-            out[:, into] = jnp.where(keep, number / total, 0.0).astype(out.dtype)
+    for head in range(heads):
+        hit = [line == r for r, h in enumerate(heads_of) if h == low + head]
+        pick = jnp.where(functools.reduce(jnp.logical_or, hit), 1.0, 0.0).astype(jnp.bfloat16)
+        total = jnp.dot(totals, pick, preferred_element_type=jnp.float32)
+        total = jnp.where(total > 0, total, 1.0)
+        cols = slice(head * HEAD_DIMENSION, (head + 1) * HEAD_DIMENSION)
+        from_own = slice(cols.start + low * HEAD_DIMENSION, cols.stop + low * HEAD_DIMENSION)
+        number = (
+            own[:BLOCK_ROWS, from_own].astype(jnp.float32)
+            + a[:BLOCK_ROWS, cols].astype(jnp.float32)
+            + b[:BLOCK_ROWS, cols].astype(jnp.float32)
+        )
+        result[:, cols] = jnp.where(keep, number / total, 0.0).astype(result.dtype)
+    copy = pltpu.make_async_copy(
+        result, out.at[:, low * HEAD_DIMENSION : (low + heads) * HEAD_DIMENSION], sem
+    )
+    copy.start()
+    copy.wait()
 
 
 SMEM = pl.BlockSpec(memory_space=pltpu.SMEM)
@@ -412,40 +435,54 @@
     swap = [(i, i ^ 1) for i in range(shards)]
     onward = [(i, i + 1) for i in range(1, shards - 1, 2)]
 
-    parts = 2
-    wide = queries.shape[1] // parts
+    second = kv_heads * SECOND_PART // 8
+    parts = [(0, kv_heads - second), (kv_heads - second, second)]
     params = pltpu.CompilerParams(vmem_limit_bytes=VMEM_LIMIT)
 
     other = send(spans, swap)
     k_other = send(keys, swap)
     v_other = send(values, swap)
-    *pieces, tail = pl.pallas_call(
+    widths = [2 * heads * HEAD_DIMENSION for _, heads in parts]
+    piece = pl.pallas_call(
+        cut_kernel,
+        out_shape=jax.ShapeDtypeStruct((BLOCK_ROWS, widths[0]), queries.dtype),
+        in_specs=[HBM],
+        out_specs=VMEM,
+        scratch_shapes=[pltpu.SemaphoreType.DMA(())],
+        compiler_params=params,
+        cost_estimate=pl.CostEstimate(flops=1, bytes_accessed=1 << 20, transcendentals=0),
+        name="cut",
+    )(in_hbm(queries))
+    rest, tail, note = pl.pallas_call(
         pack_kernel,
         out_shape=[
-            jax.ShapeDtypeStruct((BLOCK_ROWS + (NOTE_ROWS if p == 0 else 0), wide), queries.dtype)
-            for p in range(parts)
-        ]
-        + [jax.ShapeDtypeStruct((2 * reach + NOTE_ROWS, columns), keys.dtype)],
+            jax.ShapeDtypeStruct((BLOCK_ROWS, widths[1]), queries.dtype),
+            jax.ShapeDtypeStruct((2 * reach + NOTE_ROWS, columns), keys.dtype),
+            jax.ShapeDtypeStruct((8,), jnp.int32),
+        ],
         in_specs=[SMEM] * 3 + [HBM] * 3,
-        out_specs=[VMEM] * (parts + 1),
-        scratch_shapes=[pltpu.SemaphoreType.DMA((parts + 2,))],
+        out_specs=[VMEM] * 2 + [SMEM],
+        scratch_shapes=[pltpu.SemaphoreType.DMA((3,))],
         compiler_params=params,
-        cost_estimate=pl.CostEstimate(flops=1 << 20, bytes_accessed=4 << 20, transcendentals=0),
+        cost_estimate=pl.CostEstimate(flops=1, bytes_accessed=2 << 20, transcendentals=0),
         name="pack",
     )(spans, other, dirty, in_hbm(keys), in_hbm(values), in_hbm(queries))
-    near, far = [], []
-    for piece in pieces:
-        near.append(shift(piece, -back // 2))
-        far.append(shift(piece, -back))
+    pieces = [piece, rest]
+    odd_to_even = [(i, i - back // 2) for i in range(shards) if i // 2 % 2 == 1]
+    even_to_odd = [(i, i + back // 2) for i in range(shards - back // 2) if i // 2 % 2 == 0]
+    far = [shift(piece, -back) for piece in pieces]
+    near = [send(piece, odd_to_even) for piece in pieces]
+    relay = [send(piece, even_to_odd) for piece in far]
     tail = send(tail, onward)
+    near_note = shift(note, -back // 2)
+    far_note = shift(note, -back)
 
     at = index.astype(jnp.int32).reshape(1)
     angles = jnp.asarray(row_angles())
     freq = jnp.asarray(lane_frequency()[None, :])
-    part_heads = kv_heads // parts
 
     def payload(heads):
-        return jax.ShapeDtypeStruct((BLOCK_ROWS, heads * HEAD_DIMENSION + LANES), jnp.bfloat16)
+        return jax.ShapeDtypeStruct((BLOCK_ROWS + NOTE_ROWS, heads * HEAD_DIMENSION), jnp.bfloat16)
 
     by_head = pltpu.VMEM((kv_heads, 2 * rows, HEAD_DIMENSION), jnp.bfloat16)
     kr, vz, lv = pl.pallas_call(
@@ -464,19 +501,17 @@
         name="prepare",
     )(at, spans, other, angles, freq, *map(in_hbm, (keys, k_other, values, v_other)))
 
-    def visitor(kind, step, part, notes, query):
+    def visitor(kind, step, part, small, notes, query):
+        low, heads = (0, kv_heads) if part is None else parts[part]
         count = {"own": per, "middle": 2 * per, "window": per}[kind] * BLOCK_ROWS
-        heads = kv_heads if part is None else part_heads
         work = BLOCK_ROWS * 2 * heads * count
         edges = {"own": 1, "middle": 1, "window": 2}[kind]
-        extra = [*notes, tail] if kind == "window" else notes
         return pl.pallas_call(
-            functools.partial(visit_kernel, kind, step, shards, rows),
+            functools.partial(visit_kernel, kind, step, shards, rows, low),
             out_shape=payload(2 * heads),
-            in_specs=[SMEM] * 5 + [VMEM] * (6 + len(extra)),
+            in_specs=[SMEM] * (4 + len(small)) + [VMEM] * (5 + len(notes) + len(query)),
             out_specs=VMEM,
             scratch_shapes=[
-                pltpu.VMEM((BLOCK_ROWS, LANES), jnp.float32),
                 pltpu.VMEM((2 * heads, BLOCK_ROWS, HEAD_DIMENSION), jnp.bfloat16),
                 pltpu.VMEM((2 * heads, BLOCK_ROWS, HEAD_DIMENSION + LANES), jnp.float32),
                 pltpu.VMEM((edges, heads, BLOCK_ROWS, HEAD_DIMENSION), jnp.bfloat16),
@@ -487,27 +522,33 @@
             cost_estimate=pl.CostEstimate(
                 flops=work * 4 * HEAD_DIMENSION, bytes_accessed=6 << 20, transcendentals=2 * work
             ),
-        )(
-            at, jnp.full((1,), part or 0, jnp.int32), spans, other, dirty,
-            *extra, angles, freq, kr, vz, lv, query,
-        )
+        )(at, spans, other, dirty, *small, *notes, angles, freq, kr, vz, lv, *query)
 
     middle, window = [], []
-    for p in range(parts):
-        got = visitor("middle", back // 2, p, [near[0]], near[p])
+    for p in range(len(parts)):
+        got = visitor("window", back, p, [near_note, far_note], [tail], [far[p]])
+        window.append(shift(got, back))
+        got = visitor("middle", back // 2, p, [near_note], [near[p], relay[p]], [])
         middle.append(shift(got, back // 2))
-        got = visitor("window", back, p, [near[0], far[0]], far[p])
-        window.append(shift(got, back))
-    own = visitor("own", 0, None, [], queries)
-    sums = [own] + [x for p in range(parts) for x in (middle[p], window[p])]
-    return pl.pallas_call(
-        functools.partial(last_kernel, rows, parts),
-        out_shape=jax.ShapeDtypeStruct(queries.shape, queries.dtype),
-        in_specs=[SMEM] * 3 + [VMEM] * len(sums),
-        out_specs=VMEM,
-        compiler_params=params,
-        name="last",
-    )(spans, dirty, at, *sums)
+    own = visitor("own", 0, None, [], [], [queries])
+    result = []
+    for (low, heads), a, b in zip(parts, middle, window):
+        result = [
+            pl.pallas_call(
+                functools.partial(last_kernel, rows, 2 * low),
+                out_shape=jax.ShapeDtypeStruct(queries.shape, queries.dtype),
+                in_specs=[SMEM] * 3 + [VMEM] * 3 + [HBM] * len(result),
+                out_specs=HBM,
+                scratch_shapes=[
+                    pltpu.VMEM((BLOCK_ROWS, 2 * heads * HEAD_DIMENSION), queries.dtype),
+                    pltpu.SemaphoreType.DMA(()),
+                ],
+                input_output_aliases={6: 0} if result else {},
+                compiler_params=params,
+                name="last",
+            )(spans, dirty, at, own, a, b, *result)
+        ]
+    return result[0]
 
 
 def solution(mesh):

time: 117 us -> 105 us (0.90)
  the two profiles are of different devices: /device:TPU:28 before, /device:TPU:16 now
where the time goes in v2:
time: 105 us
  starting transfers between devices  43.8 us (42%)
  Pallas kernels  36.5 us (35%)
  waiting for transfers between devices  21.2 us (20%)
  local copies, waits for them, and re-layouts  1.97 us (2%)
  between operations  1.12 us (1%)
    ppermute x16, starting transfers between devices, send(): return lax.ppermute(array, 'seq', pairs)  43.8 us
    pallas_call x5, Pallas kernels, visitor(): pl.pallas_call(functools.partial(visit_kernel, kind, step, shards, rows,...  24.1 us
    ppermute x16, waiting for transfers between devices, send(): return lax.ppermute(array, 'seq', pairs)  21.2 us
    pallas_call x1, Pallas kernels, work(): pl.pallas_call(prepare_kernel, out_shape=(by_head, by_head, pltpu.VMEM((2...  4.95 us
    pallas_call x2, Pallas kernels, work(): pl.pallas_call(functools.partial(last_kernel, rows, 2 * low), out_shape=j...  3.84 us
    pallas_call x1, Pallas kernels, work(): pl.pallas_call(pack_kernel, out_shape=[jax.ShapeDtypeStruct((BLOCK_ROWS,...  2.51 us
  transfers between devices with their start and end apart: 16, of which 5 were waited for; matrix products, arithmetic and copies ran while one was open for 0% of the time, Pallas kernels for 33%

profile of v2, /device:TPU:16, one launch (start us, length us, event | category | flops | bytes accessed | tf_op | source)
XLA Modules:
  0.0 104.7 jit_solution(18297398603912467481)
XLA Ops:
  1.6 2.4 %collective-permute-start.12 = (bf16[256,1280]{1,0:T(8,128)(2,1)S(1)}, bf16[256,1280]{1,0:T(8,128)(2,1)S(1)}, u32[]{:S(2)}, u32[]{:S(2)}) collective-permute-start(bf16[256,1280]{1,0:T(8,128)(2,1)S(1)} %cut.1), channel_id=1, source_target_pairs={{4,0},{5,1},{6,2},{7,3},{8,4},{9,5},{10,6},{11,7},{12,8},{13,9},{1... | collective-permute-start | bytes 1966088 | tf_op jit(solution)/shard_map/ppermute | solution.py:43
  4.7 2.8 %collective-permute-done.other = s32[1,2]{1,0:T(1,128)S(1)} collective-permute-done((s32[1,2]{1,0:T(1,128)}, s32[1,2]{1,0:T(1,128)S(1)}, u32[]{:S(2)}, u32[]{:S(2)}) %collective-permute-start) | collective-permute-done | bytes 40 | tf_op jit(solution)/shard_map/ppermute | solution.py:43
  8.2 2.5 %pack.1 = (bf16[256,768]{1,0:T(8,128)(2,1)}, bf16[328,1024]{1,0:T(8,128)(2,1)S(1)}, s32[8]{0:T(128)S(1)}) custom-call(s32[1,2]{1,0:T(1,128)S(1)} %copy-done.2, s32[1,2]{1,0:T(1,128)S(1)} %collective-permute-done.other, s32[1]{0:T(128)S(6)} %copy.10.dirty, bf16[1024,1024]{1,0:T(8,128)(2,1)} %keys.1, bf16[1024,1024]{1,0:T(8,128)(2,1)} %values.1, ...), custom_call_target="tpu_custom_call" | custom-call | flops 1 | bytes 2097152 | tf_op jit(solution)/shard_map/pack/pallas_call | solution.py:456
  13.3 6.9 %collective-permute-done.12.refs_8_ = bf16[256,1280]{1,0:T(8,128)(2,1)S(1)} collective-permute-done((bf16[256,1280]{1,0:T(8,128)(2,1)S(1)}, bf16[256,1280]{1,0:T(8,128)(2,1)S(1)}, u32[]{:S(2)}, u32[]{:S(2)}) %collective-permute-start.12) | collective-permute-done | bytes 655392 | tf_op jit(solution)/shard_map/ppermute | solution.py:43
  20.1 4.2 %collective-permute-start.13 = (bf16[256,1280]{1,0:T(8,128)(2,1)S(1)}, bf16[256,1280]{1,0:T(8,128)(2,1)}, u32[]{:S(2)}, u32[]{:S(2)}) collective-permute-start(bf16[256,1280]{1,0:T(8,128)(2,1)S(1)} %collective-permute-done.12.refs_8_), channel_id=1, source_target_pairs={{0,2},{1,3},{4,6},{5,7},{8,10},{9,11},{12,14},{13,15},{16,18},{17,... | collective-permute-start | bytes 1966088 | tf_op jit(solution)/shard_map/ppermute | solution.py:43
  24.4 1.3 %copy-done.5 = bf16[1024,1024]{1,0:T(8,128)(2,1)} copy-done((bf16[1024,1024]{1,0:T(8,128)(2,1)}, bf16[1024,1024]{1,0:T(8,128)(2,1)S(1)}, u32[]{:S(2)}) %copy-start.5) | copy-done | bytes 2097176
  25.7 2.3 %collective-permute-start.5 = (bf16[256,768]{1,0:T(8,128)(2,1)}, bf16[256,768]{1,0:T(8,128)(2,1)S(1)}, u32[]{:S(2)}, u32[]{:S(2)}) collective-permute-start(bf16[256,768]{1,0:T(8,128)(2,1)} %get-tuple-element.15), channel_id=1, source_target_pairs={{4,0},{5,1},{6,2},{7,3},{8,4},{9,5},{10,6},{11,7},{12,8},{13,9},{1... | collective-permute-start | bytes 1179656 | tf_op jit(solution)/shard_map/ppermute | solution.py:43
  28.1 1.9 %collective-permute-start.3 = (s32[8]{0:T(128)S(1)}, s32[8]{0:T(128)S(1)}, u32[]{:S(2)}, u32[]{:S(2)}) collective-permute-start(s32[8]{0:T(128)S(1)} %get-tuple-element.14), channel_id=1, source_target_pairs={{2,0},{3,1},{4,2},{5,3},{6,4},{7,5},{8,6},{9,7},{10,8},{11,9},{12,... | collective-permute-start | bytes 104 | tf_op jit(solution)/shard_map/ppermute | solution.py:43
  30.0 4.9 %prepare.1 = (bf16[8,2048,128]{2,1,0:T(8,128)(2,1)S(1)}, bf16[8,2048,128]{2,1,0:T(8,128)(2,1)S(1)}, bf16[2048,128]{1,0:T(8,128)(2,1)S(1)}) custom-call(s32[1]{0:T(128)} %bitcast.index_ref, s32[1,2]{1,0:T(1,128)S(1)} %copy-done.3, s32[1,2]{1,0:T(1,128)S(1)} %collective-permute-done.other, f32[2,256,128]{2,1,0:T(8,128)S(1)} %copy-done.1, ...), custom_call_target="tpu_custom_call" | custom-call | flops 16777216 | bytes 20971520 | tf_op jit(solution)/shard_map/prepare/pallas_call | solution.py:488
  35.0 2.7 %collective-permute-done.3.refs_0_ = s32[8]{0:T(128)S(1)} collective-permute-done((s32[8]{0:T(128)S(1)}, s32[8]{0:T(128)S(1)}, u32[]{:S(2)}, u32[]{:S(2)}) %collective-permute-start.3) | collective-permute-done | bytes 64 | tf_op jit(solution)/shard_map/ppermute | solution.py:43
  37.7 2.3 %collective-permute-start.8 = (s32[8]{0:T(128)S(1)}, s32[8]{0:T(128)S(1)}, u32[]{:S(2)}, u32[]{:S(2)}) collective-permute-start(s32[8]{0:T(128)S(1)} %get-tuple-element.14), channel_id=1, source_target_pairs={{4,0},{5,1},{6,2},{7,3},{8,4},{9,5},{10,6},{11,7},{12,8},{13,9},{1... | collective-permute-start | bytes 104 | tf_op jit(solution)/shard_map/ppermute | solution.py:43
  40.1 3.1 %collective-permute-done.8.refs_1_ = s32[8]{0:T(128)S(1)} collective-permute-done((s32[8]{0:T(128)S(1)}, s32[8]{0:T(128)S(1)}, u32[]{:S(2)}, u32[]{:S(2)}) %collective-permute-start.8) | collective-permute-done | bytes 64 | tf_op jit(solution)/shard_map/ppermute | solution.py:43
  44.5 4.6 %collective-permute-start.6 = (bf16[256,768]{1,0:T(8,128)(2,1)S(1)}, bf16[256,768]{1,0:T(8,128)(2,1)S(1)}, u32[]{:S(2)}, u32[]{:S(2)}) collective-permute-start(bf16[256,768]{1,0:T(8,128)(2,1)S(1)} %collective-permute-done.5.refs_8_), channel_id=1, source_target_pairs={{0,2},{1,3},{4,6},{5,7},{8,10},{9,11},{12,14},{13,15},{16,18},{17,... | collective-permute-start | bytes 1179656 | tf_op jit(solution)/shard_map/ppermute | solution.py:43
  49.1 9.1 %shard_map.77 = bf16[264,1280]{1,0:T(8,128)(2,1)S(1)} custom-call(s32[1]{0:T(128)} %bitcast.index_ref, s32[1,2]{1,0:T(1,128)S(1)} %copy-done.3, s32[1,2]{1,0:T(1,128)S(1)} %collective-permute-done.other, s32[1]{0:T(128)S(6)} %copy.10.dirty, s32[8]{0:T(128)S(1)} %collective-permute-done.3.refs_0_, s32[8]{0:T(128)S(1)} %collective-permute-done.8.refs_1_, ...), custom_call_target="tpu_custom_call" | custom-call | flops 1342177280 | bytes 6291456 | tf_op jit(solution)/shard_map/pallas_call | solution.py:509
  58.2 1.9 %collective-permute-start.15 = (bf16[264,1280]{1,0:T(8,128)(2,1)S(1)}, bf16[264,1280]{1,0:T(8,128)(2,1)S(1)}, u32[]{:S(2)}, u32[]{:S(2)}) collective-permute-start(bf16[264,1280]{1,0:T(8,128)(2,1)S(1)} %shard_map.77), channel_id=1, source_target_pairs={{0,4},{1,5},{2,6},{3,7},{4,8},{5,9},{6,10},{7,11},{8,12},{9,13},{1... | collective-permute-start | bytes 2027528 | tf_op jit(solution)/shard_map/ppermute | solution.py:43
  60.2 1.4 %shard_map.76 = bf16[264,1280]{1,0:T(8,128)(2,1)S(1)} custom-call(s32[1]{0:T(128)} %bitcast.index_ref, s32[1,2]{1,0:T(1,128)S(1)} %copy-done.3, s32[1,2]{1,0:T(1,128)S(1)} %collective-permute-done.other, s32[1]{0:T(128)S(6)} %copy.10.dirty, s32[8]{0:T(128)S(1)} %collective-permute-done.3.refs_0_, bf16[256,1280]{1,0:T(8,128)(2,1)} %collective-permute-done.11.refs_1_, ...), custom_call_target="tpu_custom_call" | custom-call | flops 2684354560 | bytes 6291456 | tf_op jit(solution)/shard_map/pallas_call | solution.py:509
  61.5 10.0 %collective-permute-start.14 = (bf16[264,1280]{1,0:T(8,128)(2,1)S(1)}, bf16[264,1280]{1,0:T(8,128)(2,1)S(1)}, u32[]{:S(2)}, u32[]{:S(2)}) collective-permute-start(bf16[264,1280]{1,0:T(8,128)(2,1)S(1)} %shard_map.76), channel_id=1, source_target_pairs={{0,2},{1,3},{2,4},{3,5},{4,6},{5,7},{6,8},{7,9},{8,10},{9,11},{10,... | collective-permute-start | bytes 2027528 | tf_op jit(solution)/shard_map/ppermute | solution.py:43
  71.6 6.1 %shard_map.75 = bf16[264,768]{1,0:T(8,128)(2,1)S(1)} custom-call(s32[1]{0:T(128)} %bitcast.index_ref, s32[1,2]{1,0:T(1,128)S(1)} %copy-done.3, s32[1,2]{1,0:T(1,128)S(1)} %collective-permute-done.other, s32[1]{0:T(128)S(6)} %copy.10.dirty, s32[8]{0:T(128)S(1)} %collective-permute-done.3.refs_0_, s32[8]{0:T(128)S(1)} %collective-permute-done.8.refs_1_, ...), custom_call_target="tpu_custom_call" | custom-call | flops 805306368 | bytes 6291456 | tf_op jit(solution)/shard_map/pallas_call | solution.py:509
  77.7 2.2 %collective-permute-start.10 = (bf16[264,768]{1,0:T(8,128)(2,1)S(1)}, bf16[264,768]{1,0:T(8,128)(2,1)S(1)}, u32[]{:S(2)}, u32[]{:S(2)}) collective-permute-start(bf16[264,768]{1,0:T(8,128)(2,1)S(1)} %shard_map.75), channel_id=1, source_target_pairs={{0,4},{1,5},{2,6},{3,7},{4,8},{5,9},{6,10},{7,11},{8,12},{9,13},{1... | collective-permute-start | bytes 1216520 | tf_op jit(solution)/shard_map/ppermute | solution.py:43
  80.6 7.4 %collective-permute-start.7 = (bf16[264,768]{1,0:T(8,128)(2,1)S(1)}, bf16[264,768]{1,0:T(8,128)(2,1)S(1)}, u32[]{:S(2)}, u32[]{:S(2)}) collective-permute-start(bf16[264,768]{1,0:T(8,128)(2,1)S(1)} %shard_map.74), channel_id=1, source_target_pairs={{0,2},{1,3},{2,4},{3,5},{4,6},{5,7},{6,8},{7,9},{8,10},{9,11},{10,... | collective-permute-start | bytes 1216520 | tf_op jit(solution)/shard_map/ppermute | solution.py:43
  88.0 6.9 %shard_map.73.own = bf16[264,2048]{1,0:T(8,128)(2,1)S(1)} custom-call(s32[1]{0:T(128)} %bitcast.index_ref, s32[1,2]{1,0:T(1,128)S(1)} %copy-done.3, s32[1,2]{1,0:T(1,128)S(1)} %collective-permute-done.other, s32[1]{0:T(128)S(6)} %copy.10.dirty, f32[2,256,128]{2,1,0:T(8,128)S(1)} %copy-done.1, f32[1,128]{1,0:T(1,128)S(1)} %copy-done.4, ...), custom_call_target="tpu_custom_call" | custom-call | flops 2147483648 | bytes 6291456 | tf_op jit(solution)/shard_map/pallas_call | solution.py:509
  94.9 2.1 %last.2.refs_0_ = bf16[256,2048]{1,0:T(8,128)(2,1)} custom-call(s32[1,2]{1,0:T(1,128)S(1)} %copy-done.3, s32[1]{0:T(128)S(6)} %copy.10.dirty, s32[1]{0:T(128)} %bitcast.index_ref, bf16[264,2048]{1,0:T(8,128)(2,1)S(1)} %shard_map.73.own, bf16[264,1280]{1,0:T(8,128)(2,1)S(1)} %collective-permute-done.14.a, bf16[264,1280]{1,0:T(8,128)(2,1)S(1)} %collective-permute-done.15.b), custom_call_target="tpu_custom_call" | custom-call | tf_op jit(solution)/shard_map/last/pallas_call | solution.py:537
  97.0 5.7 %collective-permute-done.7.a = bf16[264,768]{1,0:T(8,128)(2,1)S(1)} collective-permute-done((bf16[264,768]{1,0:T(8,128)(2,1)S(1)}, bf16[264,768]{1,0:T(8,128)(2,1)S(1)}, u32[]{:S(2)}, u32[]{:S(2)}) %collective-permute-start.7) | collective-permute-done | bytes 405536 | tf_op jit(solution)/shard_map/ppermute | solution.py:43
  102.7 1.8 %last.3 = bf16[256,2048]{1,0:T(8,128)(2,1)} custom-call(s32[1,2]{1,0:T(1,128)S(1)} %copy-done.3, s32[1]{0:T(128)S(6)} %copy.10.dirty, s32[1]{0:T(128)} %bitcast.index_ref, bf16[264,2048]{1,0:T(8,128)(2,1)S(1)} %shard_map.73.own, bf16[264,768]{1,0:T(8,128)(2,1)S(1)} %collective-permute-done.7.a, ...), custom_call_target="tpu_custom_call", output_to_operand_aliasing={{}: (6, {})} | custom-call | tf_op jit(solution)/shard_map/last/pallas_call | solution.py:537
  (30 shorter events, 6.8 us)
Async XLA Ops:
  0.0 24.4 %collective-permute-start.1 = (bf16[1024,1024]{1,0:T(8,128)(2,1)}, bf16[1024,1024]{1,0:T(8,128)(2,1)S(1)}, u32[]{:S(2)}, u32[]{:S(2)}) collective-permute-start(bf16[1024,1024]{1,0:T(8,128)(2,1)} %keys.1), channel_id=1, source_target_pairs={{0,1},{1,0},{2,3},{3,2},{4,5},{5,4},{6,7},{7,6},{8,9},{9,8},{10,11... | collective-permute-start | bytes 6291464 | tf_op jit(solution)/shard_map/ppermute | solution.py:43
  0.0 28.1 %collective-permute-start.2 = (bf16[1024,1024]{1,0:T(8,128)(2,1)}, bf16[1024,1024]{1,0:T(8,128)(2,1)}, u32[]{:S(2)}, u32[]{:S(2)}) collective-permute-start(bf16[1024,1024]{1,0:T(8,128)(2,1)} %values.1), channel_id=1, source_target_pairs={{0,1},{1,0},{2,3},{3,2},{4,5},{5,4},{6,7},{7,6},{8,9},{9,8},{10,11... | collective-permute-start | bytes 6291464 | tf_op jit(solution)/shard_map/ppermute | solution.py:43
  1.6 18.5 %collective-permute-start.12 = (bf16[256,1280]{1,0:T(8,128)(2,1)S(1)}, bf16[256,1280]{1,0:T(8,128)(2,1)S(1)}, u32[]{:S(2)}, u32[]{:S(2)}) collective-permute-start(bf16[256,1280]{1,0:T(8,128)(2,1)S(1)} %cut.1), channel_id=1, source_target_pairs={{4,0},{5,1},{6,2},{7,3},{8,4},{9,5},{10,6},{11,7},{12,8},{13,9},{1... | collective-permute-start | bytes 1966088 | tf_op jit(solution)/shard_map/ppermute | solution.py:43
  4.0 3.5 %collective-permute-start = (s32[1,2]{1,0:T(1,128)}, s32[1,2]{1,0:T(1,128)S(1)}, u32[]{:S(2)}, u32[]{:S(2)}) collective-permute-start(s32[1,2]{1,0:T(1,128)} %spans.17), channel_id=1, source_target_pairs={{0,1},{1,0},{2,3},{3,2},{4,5},{5,4},{6,7},{7,6},{8,9},{9,8},{10,11... | collective-permute-start | bytes 32 | tf_op jit(solution)/shard_map/ppermute | solution.py:43
  4.7 25.3 %copy-start.1 = (f32[2,256,128]{2,1,0:T(8,128)S(1)}, f32[2,256,128]{2,1,0:T(8,128)}, u32[]{:S(2)}) copy-start(f32[2,256,128]{2,1,0:T(8,128)} %constant.8.clone.angles.refs_0_.refs_3_) | copy-start | bytes 786436
  7.5 0.7 copy-start.2
  8.2 21.8 %copy-start.3 = (s32[1,2]{1,0:T(1,128)S(1)}, s32[1,2]{1,0:T(1,128)}, u32[]{:S(2)}) copy-start(s32[1,2]{1,0:T(1,128)} %spans.17) | copy-start | bytes 28
  8.2 21.9 %copy-start.4 = (f32[1,128]{1,0:T(1,128)S(1)}, f32[1,128]{1,0:T(1,128)}, u32[]{:S(2)}) copy-start(f32[1,128]{1,0:T(1,128)} %constant.9.clone.freq.refs_1_.refs_4_) | copy-start | bytes 1540
  10.7 38.4 %collective-permute-start.9 = (bf16[328,1024]{1,0:T(8,128)(2,1)S(1)}, bf16[328,1024]{1,0:T(8,128)(2,1)S(1)}, u32[]{:S(2)}, u32[]{:S(2)}) collective-permute-start(bf16[328,1024]{1,0:T(8,128)(2,1)S(1)} %get-tuple-element.16), channel_id=1, source_target_pairs={{1,2},{3,4},{5,6},{7,8},{9,10},{11,12},{13,14},{17,18},{19,20},{21... | collective-permute-start | bytes 2015240 | tf_op jit(solution)/shard_map/ppermute | solution.py:43
  12.0 48.2 %collective-permute-start.11 = (bf16[256,1280]{1,0:T(8,128)(2,1)S(1)}, bf16[256,1280]{1,0:T(8,128)(2,1)}, u32[]{:S(2)}, u32[]{:S(2)}) collective-permute-start(bf16[256,1280]{1,0:T(8,128)(2,1)S(1)} %cut.1), channel_id=1, source_target_pairs={{2,0},{3,1},{6,4},{7,5},{10,8},{11,9},{14,12},{15,13},{18,16},{19,... | collective-permute-start | bytes 1966088 | tf_op jit(solution)/shard_map/ppermute | solution.py:43
  20.1 40.0 %collective-permute-start.13 = (bf16[256,1280]{1,0:T(8,128)(2,1)S(1)}, bf16[256,1280]{1,0:T(8,128)(2,1)}, u32[]{:S(2)}, u32[]{:S(2)}) collective-permute-start(bf16[256,1280]{1,0:T(8,128)(2,1)S(1)} %collective-permute-done.12.refs_8_), channel_id=1, source_target_pairs={{0,2},{1,3},{4,6},{5,7},{8,10},{9,11},{12,14},{13,15},{16,18},{17,... | collective-permute-start | bytes 1966088 | tf_op jit(solution)/shard_map/ppermute | solution.py:43
  24.4 1.3 %copy-start.5 = (bf16[1024,1024]{1,0:T(8,128)(2,1)}, bf16[1024,1024]{1,0:T(8,128)(2,1)S(1)}, u32[]{:S(2)}) copy-start(bf16[1024,1024]{1,0:T(8,128)(2,1)S(1)} %collective-permute-done.1.k_other) | copy-start | bytes 6291460
  25.7 18.8 %collective-permute-start.5 = (bf16[256,768]{1,0:T(8,128)(2,1)}, bf16[256,768]{1,0:T(8,128)(2,1)S(1)}, u32[]{:S(2)}, u32[]{:S(2)}) collective-permute-start(bf16[256,768]{1,0:T(8,128)(2,1)} %get-tuple-element.15), channel_id=1, source_target_pairs={{4,0},{5,1},{6,2},{7,3},{8,4},{9,5},{10,6},{11,7},{12,8},{13,9},{1... | collective-permute-start | bytes 1179656 | tf_op jit(solution)/shard_map/ppermute | solution.py:43
  28.1 9.7 %collective-permute-start.3 = (s32[8]{0:T(128)S(1)}, s32[8]{0:T(128)S(1)}, u32[]{:S(2)}, u32[]{:S(2)}) collective-permute-start(s32[8]{0:T(128)S(1)} %get-tuple-element.14), channel_id=1, source_target_pairs={{2,0},{3,1},{4,2},{5,3},{6,4},{7,5},{8,6},{9,7},{10,8},{11,9},{12,... | collective-permute-start | bytes 104 | tf_op jit(solution)/shard_map/ppermute | solution.py:43
  37.7 5.5 %collective-permute-start.8 = (s32[8]{0:T(128)S(1)}, s32[8]{0:T(128)S(1)}, u32[]{:S(2)}, u32[]{:S(2)}) collective-permute-start(s32[8]{0:T(128)S(1)} %get-tuple-element.14), channel_id=1, source_target_pairs={{4,0},{5,1},{6,2},{7,3},{8,4},{9,5},{10,6},{11,7},{12,8},{13,9},{1... | collective-permute-start | bytes 104 | tf_op jit(solution)/shard_map/ppermute | solution.py:43
  43.2 36.8 %collective-permute-start.4 = (bf16[256,768]{1,0:T(8,128)(2,1)}, bf16[256,768]{1,0:T(8,128)(2,1)S(1)}, u32[]{:S(2)}, u32[]{:S(2)}) collective-permute-start(bf16[256,768]{1,0:T(8,128)(2,1)} %get-tuple-element.15), channel_id=1, source_target_pairs={{2,0},{3,1},{6,4},{7,5},{10,8},{11,9},{14,12},{15,13},{18,16},{19,... | collective-permute-start | bytes 1179656 | tf_op jit(solution)/shard_map/ppermute | solution.py:43
  44.5 35.5 %collective-permute-start.6 = (bf16[256,768]{1,0:T(8,128)(2,1)S(1)}, bf16[256,768]{1,0:T(8,128)(2,1)S(1)}, u32[]{:S(2)}, u32[]{:S(2)}) collective-permute-start(bf16[256,768]{1,0:T(8,128)(2,1)S(1)} %collective-permute-done.5.refs_8_), channel_id=1, source_target_pairs={{0,2},{1,3},{4,6},{5,7},{8,10},{9,11},{12,14},{13,15},{16,18},{17,... | collective-permute-start | bytes 1179656 | tf_op jit(solution)/shard_map/ppermute | solution.py:43
  58.2 36.7 %collective-permute-start.15 = (bf16[264,1280]{1,0:T(8,128)(2,1)S(1)}, bf16[264,1280]{1,0:T(8,128)(2,1)S(1)}, u32[]{:S(2)}, u32[]{:S(2)}) collective-permute-start(bf16[264,1280]{1,0:T(8,128)(2,1)S(1)} %shard_map.77), channel_id=1, source_target_pairs={{0,4},{1,5},{2,6},{3,7},{4,8},{5,9},{6,10},{7,11},{8,12},{9,13},{1... | collective-permute-start | bytes 2027528 | tf_op jit(solution)/shard_map/ppermute | solution.py:43
  61.5 33.4 %collective-permute-start.14 = (bf16[264,1280]{1,0:T(8,128)(2,1)S(1)}, bf16[264,1280]{1,0:T(8,128)(2,1)S(1)}, u32[]{:S(2)}, u32[]{:S(2)}) collective-permute-start(bf16[264,1280]{1,0:T(8,128)(2,1)S(1)} %shard_map.76), channel_id=1, source_target_pairs={{0,2},{1,3},{2,4},{3,5},{4,6},{5,7},{6,8},{7,9},{8,10},{9,11},{10,... | collective-permute-start | bytes 2027528 | tf_op jit(solution)/shard_map/ppermute | solution.py:43
  77.7 10.3 %copy-start = (bf16[256,2048]{1,0:T(8,128)(2,1)S(1)}, bf16[256,2048]{1,0:T(8,128)(2,1)}, u32[]{:S(2)}) copy-start(bf16[256,2048]{1,0:T(8,128)(2,1)} %query.3) | copy-start | bytes 3145732
  77.7 19.3 %collective-permute-start.10 = (bf16[264,768]{1,0:T(8,128)(2,1)S(1)}, bf16[264,768]{1,0:T(8,128)(2,1)S(1)}, u32[]{:S(2)}, u32[]{:S(2)}) collective-permute-start(bf16[264,768]{1,0:T(8,128)(2,1)S(1)} %shard_map.75), channel_id=1, source_target_pairs={{0,4},{1,5},{2,6},{3,7},{4,8},{5,9},{6,10},{7,11},{8,12},{9,13},{1... | collective-permute-start | bytes 1216520 | tf_op jit(solution)/shard_map/ppermute | solution.py:43
  80.6 22.2 %collective-permute-start.7 = (bf16[264,768]{1,0:T(8,128)(2,1)S(1)}, bf16[264,768]{1,0:T(8,128)(2,1)S(1)}, u32[]{:S(2)}, u32[]{:S(2)}) collective-permute-start(bf16[264,768]{1,0:T(8,128)(2,1)S(1)} %shard_map.74), channel_id=1, source_target_pairs={{0,2},{1,3},{2,4},{3,5},{4,6},{5,7},{6,8},{7,9},{8,10},{9,11},{10,... | collective-permute-start | bytes 1216520 | tf_op jit(solution)/shard_map/ppermute | solution.py:43

commit v3 on v2

--- a/solution.py
+++ b/solution.py
@@ -224,8 +224,13 @@
                 ve[0, i] = jnp.concatenate([zero, tail_v[:, cols]], axis=0) * le[0]
 
         stage(1, first)
-        before = places_at(block - 1)
-        before = jnp.where(first == 0, places(tail_tile, 1, (1, BLOCK_ROWS)), before)
+        inside = block > 0
+        row = jnp.where(inside, block - 1, per - 1) * BLOCK_ROWS
+        last = frame.tile(0, (per - 1) * BLOCK_ROWS)
+        even = [jnp.where(inside, a, b) for a, b in zip(frame.tile(0, row), tail_tile)]
+        other = [jnp.where(inside, a, b) for a, b in zip(frame.tile(1, row), last)]
+        tile = [jnp.where(odd == 1, b, a) for a, b in zip(even, other)]
+        before = places(tile, 1, (1, BLOCK_ROWS))
         masked(0, own - before < WINDOW, True)
         masked(1, own - places_at(block) < WINDOW, False)
 

time: 105 us -> 105 us (level)
  no operation moved by 1% of the time
where the time goes in v3:
time: 105 us
  starting transfers between devices  43.8 us (42%)
  Pallas kernels  36.5 us (35%)
  waiting for transfers between devices  21.2 us (20%)
  local copies, waits for them, and re-layouts  1.97 us (2%)
  between operations  1.12 us (1%)
    ppermute x16, starting transfers between devices, send(): return lax.ppermute(array, 'seq', pairs)  43.8 us
    pallas_call x5, Pallas kernels, visitor(): pl.pallas_call(functools.partial(visit_kernel, kind, step, shards, rows,...  24.1 us
    ppermute x16, waiting for transfers between devices, send(): return lax.ppermute(array, 'seq', pairs)  21.2 us
    pallas_call x1, Pallas kernels, work(): pl.pallas_call(prepare_kernel, out_shape=(by_head, by_head, pltpu.VMEM((2...  4.95 us
    pallas_call x2, Pallas kernels, work(): pl.pallas_call(functools.partial(last_kernel, rows, 2 * low), out_shape=j...  3.84 us
    pallas_call x1, Pallas kernels, work(): pl.pallas_call(pack_kernel, out_shape=[jax.ShapeDtypeStruct((BLOCK_ROWS,...  2.51 us
  transfers between devices with their start and end apart: 16, of which 5 were waited for; matrix products, arithmetic and copies ran while one was open for 0% of the time, Pallas kernels for 33%

profile of v3, /device:TPU:16, one launch (start us, length us, event | category | flops | bytes accessed | tf_op | source)
XLA Modules:
  0.0 104.7 jit_solution(6922361697231850839)
XLA Ops:
  1.6 2.4 %collective-permute-start.12 = (bf16[256,1280]{1,0:T(8,128)(2,1)S(1)}, bf16[256,1280]{1,0:T(8,128)(2,1)S(1)}, u32[]{:S(2)}, u32[]{:S(2)}) collective-permute-start(bf16[256,1280]{1,0:T(8,128)(2,1)S(1)} %cut.1), channel_id=1, source_target_pairs={{4,0},{5,1},{6,2},{7,3},{8,4},{9,5},{10,6},{11,7},{12,8},{13,9},{1... | collective-permute-start | bytes 1966088 | tf_op jit(solution)/shard_map/ppermute | solution.py:43
  4.7 2.8 %collective-permute-done.other = s32[1,2]{1,0:T(1,128)S(1)} collective-permute-done((s32[1,2]{1,0:T(1,128)}, s32[1,2]{1,0:T(1,128)S(1)}, u32[]{:S(2)}, u32[]{:S(2)}) %collective-permute-start) | collective-permute-done | bytes 40 | tf_op jit(solution)/shard_map/ppermute | solution.py:43
  8.2 2.5 %pack.1 = (bf16[256,768]{1,0:T(8,128)(2,1)}, bf16[328,1024]{1,0:T(8,128)(2,1)S(1)}, s32[8]{0:T(128)S(1)}) custom-call(s32[1,2]{1,0:T(1,128)S(1)} %copy-done.2, s32[1,2]{1,0:T(1,128)S(1)} %collective-permute-done.other, s32[1]{0:T(128)S(6)} %copy.10.dirty, bf16[1024,1024]{1,0:T(8,128)(2,1)} %keys.1, bf16[1024,1024]{1,0:T(8,128)(2,1)} %values.1, ...), custom_call_target="tpu_custom_call" | custom-call | flops 1 | bytes 2097152 | tf_op jit(solution)/shard_map/pack/pallas_call | solution.py:461
  13.3 6.9 %collective-permute-done.12.refs_8_ = bf16[256,1280]{1,0:T(8,128)(2,1)S(1)} collective-permute-done((bf16[256,1280]{1,0:T(8,128)(2,1)S(1)}, bf16[256,1280]{1,0:T(8,128)(2,1)S(1)}, u32[]{:S(2)}, u32[]{:S(2)}) %collective-permute-start.12) | collective-permute-done | bytes 655392 | tf_op jit(solution)/shard_map/ppermute | solution.py:43
  20.1 4.2 %collective-permute-start.13 = (bf16[256,1280]{1,0:T(8,128)(2,1)S(1)}, bf16[256,1280]{1,0:T(8,128)(2,1)}, u32[]{:S(2)}, u32[]{:S(2)}) collective-permute-start(bf16[256,1280]{1,0:T(8,128)(2,1)S(1)} %collective-permute-done.12.refs_8_), channel_id=1, source_target_pairs={{0,2},{1,3},{4,6},{5,7},{8,10},{9,11},{12,14},{13,15},{16,18},{17,... | collective-permute-start | bytes 1966088 | tf_op jit(solution)/shard_map/ppermute | solution.py:43
  24.4 1.3 %copy-done.5 = bf16[1024,1024]{1,0:T(8,128)(2,1)} copy-done((bf16[1024,1024]{1,0:T(8,128)(2,1)}, bf16[1024,1024]{1,0:T(8,128)(2,1)S(1)}, u32[]{:S(2)}) %copy-start.5) | copy-done | bytes 2097176
  25.7 2.3 %collective-permute-start.5 = (bf16[256,768]{1,0:T(8,128)(2,1)}, bf16[256,768]{1,0:T(8,128)(2,1)S(1)}, u32[]{:S(2)}, u32[]{:S(2)}) collective-permute-start(bf16[256,768]{1,0:T(8,128)(2,1)} %get-tuple-element.15), channel_id=1, source_target_pairs={{4,0},{5,1},{6,2},{7,3},{8,4},{9,5},{10,6},{11,7},{12,8},{13,9},{1... | collective-permute-start | bytes 1179656 | tf_op jit(solution)/shard_map/ppermute | solution.py:43
  28.1 1.9 %collective-permute-start.3 = (s32[8]{0:T(128)S(1)}, s32[8]{0:T(128)S(1)}, u32[]{:S(2)}, u32[]{:S(2)}) collective-permute-start(s32[8]{0:T(128)S(1)} %get-tuple-element.14), channel_id=1, source_target_pairs={{2,0},{3,1},{4,2},{5,3},{6,4},{7,5},{8,6},{9,7},{10,8},{11,9},{12,... | collective-permute-start | bytes 104 | tf_op jit(solution)/shard_map/ppermute | solution.py:43
  30.0 4.9 %prepare.1 = (bf16[8,2048,128]{2,1,0:T(8,128)(2,1)S(1)}, bf16[8,2048,128]{2,1,0:T(8,128)(2,1)S(1)}, bf16[2048,128]{1,0:T(8,128)(2,1)S(1)}) custom-call(s32[1]{0:T(128)} %bitcast.index_ref, s32[1,2]{1,0:T(1,128)S(1)} %copy-done.3, s32[1,2]{1,0:T(1,128)S(1)} %collective-permute-done.other, f32[2,256,128]{2,1,0:T(8,128)S(1)} %copy-done.1, ...), custom_call_target="tpu_custom_call" | custom-call | flops 16777216 | bytes 20971520 | tf_op jit(solution)/shard_map/prepare/pallas_call | solution.py:493
  35.0 2.7 %collective-permute-done.3.refs_0_ = s32[8]{0:T(128)S(1)} collective-permute-done((s32[8]{0:T(128)S(1)}, s32[8]{0:T(128)S(1)}, u32[]{:S(2)}, u32[]{:S(2)}) %collective-permute-start.3) | collective-permute-done | bytes 64 | tf_op jit(solution)/shard_map/ppermute | solution.py:43
  37.7 2.3 %collective-permute-start.8 = (s32[8]{0:T(128)S(1)}, s32[8]{0:T(128)S(1)}, u32[]{:S(2)}, u32[]{:S(2)}) collective-permute-start(s32[8]{0:T(128)S(1)} %get-tuple-element.14), channel_id=1, source_target_pairs={{4,0},{5,1},{6,2},{7,3},{8,4},{9,5},{10,6},{11,7},{12,8},{13,9},{1... | collective-permute-start | bytes 104 | tf_op jit(solution)/shard_map/ppermute | solution.py:43
  40.1 3.1 %collective-permute-done.8.refs_1_ = s32[8]{0:T(128)S(1)} collective-permute-done((s32[8]{0:T(128)S(1)}, s32[8]{0:T(128)S(1)}, u32[]{:S(2)}, u32[]{:S(2)}) %collective-permute-start.8) | collective-permute-done | bytes 64 | tf_op jit(solution)/shard_map/ppermute | solution.py:43
  44.5 4.6 %collective-permute-start.6 = (bf16[256,768]{1,0:T(8,128)(2,1)S(1)}, bf16[256,768]{1,0:T(8,128)(2,1)S(1)}, u32[]{:S(2)}, u32[]{:S(2)}) collective-permute-start(bf16[256,768]{1,0:T(8,128)(2,1)S(1)} %collective-permute-done.5.refs_8_), channel_id=1, source_target_pairs={{0,2},{1,3},{4,6},{5,7},{8,10},{9,11},{12,14},{13,15},{16,18},{17,... | collective-permute-start | bytes 1179656 | tf_op jit(solution)/shard_map/ppermute | solution.py:43
  49.1 9.1 %shard_map.77 = bf16[264,1280]{1,0:T(8,128)(2,1)S(1)} custom-call(s32[1]{0:T(128)} %bitcast.index_ref, s32[1,2]{1,0:T(1,128)S(1)} %copy-done.3, s32[1,2]{1,0:T(1,128)S(1)} %collective-permute-done.other, s32[1]{0:T(128)S(6)} %copy.10.dirty, s32[8]{0:T(128)S(1)} %collective-permute-done.3.refs_0_, s32[8]{0:T(128)S(1)} %collective-permute-done.8.refs_1_, ...), custom_call_target="tpu_custom_call" | custom-call | flops 1342177280 | bytes 6291456 | tf_op jit(solution)/shard_map/pallas_call | solution.py:514
  58.2 1.9 %collective-permute-start.15 = (bf16[264,1280]{1,0:T(8,128)(2,1)S(1)}, bf16[264,1280]{1,0:T(8,128)(2,1)S(1)}, u32[]{:S(2)}, u32[]{:S(2)}) collective-permute-start(bf16[264,1280]{1,0:T(8,128)(2,1)S(1)} %shard_map.77), channel_id=1, source_target_pairs={{0,4},{1,5},{2,6},{3,7},{4,8},{5,9},{6,10},{7,11},{8,12},{9,13},{1... | collective-permute-start | bytes 2027528 | tf_op jit(solution)/shard_map/ppermute | solution.py:43
  60.2 1.4 %shard_map.76 = bf16[264,1280]{1,0:T(8,128)(2,1)S(1)} custom-call(s32[1]{0:T(128)} %bitcast.index_ref, s32[1,2]{1,0:T(1,128)S(1)} %copy-done.3, s32[1,2]{1,0:T(1,128)S(1)} %collective-permute-done.other, s32[1]{0:T(128)S(6)} %copy.10.dirty, s32[8]{0:T(128)S(1)} %collective-permute-done.3.refs_0_, bf16[256,1280]{1,0:T(8,128)(2,1)} %collective-permute-done.11.refs_1_, ...), custom_call_target="tpu_custom_call" | custom-call | flops 2684354560 | bytes 6291456 | tf_op jit(solution)/shard_map/pallas_call | solution.py:514
  61.5 10.0 %collective-permute-start.14 = (bf16[264,1280]{1,0:T(8,128)(2,1)S(1)}, bf16[264,1280]{1,0:T(8,128)(2,1)S(1)}, u32[]{:S(2)}, u32[]{:S(2)}) collective-permute-start(bf16[264,1280]{1,0:T(8,128)(2,1)S(1)} %shard_map.76), channel_id=1, source_target_pairs={{0,2},{1,3},{2,4},{3,5},{4,6},{5,7},{6,8},{7,9},{8,10},{9,11},{10,... | collective-permute-start | bytes 2027528 | tf_op jit(solution)/shard_map/ppermute | solution.py:43
  71.6 6.1 %shard_map.75 = bf16[264,768]{1,0:T(8,128)(2,1)S(1)} custom-call(s32[1]{0:T(128)} %bitcast.index_ref, s32[1,2]{1,0:T(1,128)S(1)} %copy-done.3, s32[1,2]{1,0:T(1,128)S(1)} %collective-permute-done.other, s32[1]{0:T(128)S(6)} %copy.10.dirty, s32[8]{0:T(128)S(1)} %collective-permute-done.3.refs_0_, s32[8]{0:T(128)S(1)} %collective-permute-done.8.refs_1_, ...), custom_call_target="tpu_custom_call" | custom-call | flops 805306368 | bytes 6291456 | tf_op jit(solution)/shard_map/pallas_call | solution.py:514
  77.7 2.2 %collective-permute-start.10 = (bf16[264,768]{1,0:T(8,128)(2,1)S(1)}, bf16[264,768]{1,0:T(8,128)(2,1)S(1)}, u32[]{:S(2)}, u32[]{:S(2)}) collective-permute-start(bf16[264,768]{1,0:T(8,128)(2,1)S(1)} %shard_map.75), channel_id=1, source_target_pairs={{0,4},{1,5},{2,6},{3,7},{4,8},{5,9},{6,10},{7,11},{8,12},{9,13},{1... | collective-permute-start | bytes 1216520 | tf_op jit(solution)/shard_map/ppermute | solution.py:43
  80.6 7.4 %collective-permute-start.7 = (bf16[264,768]{1,0:T(8,128)(2,1)S(1)}, bf16[264,768]{1,0:T(8,128)(2,1)S(1)}, u32[]{:S(2)}, u32[]{:S(2)}) collective-permute-start(bf16[264,768]{1,0:T(8,128)(2,1)S(1)} %shard_map.74), channel_id=1, source_target_pairs={{0,2},{1,3},{2,4},{3,5},{4,6},{5,7},{6,8},{7,9},{8,10},{9,11},{10,... | collective-permute-start | bytes 1216520 | tf_op jit(solution)/shard_map/ppermute | solution.py:43
  88.0 6.9 %shard_map.73.own = bf16[264,2048]{1,0:T(8,128)(2,1)S(1)} custom-call(s32[1]{0:T(128)} %bitcast.index_ref, s32[1,2]{1,0:T(1,128)S(1)} %copy-done.3, s32[1,2]{1,0:T(1,128)S(1)} %collective-permute-done.other, s32[1]{0:T(128)S(6)} %copy.10.dirty, f32[2,256,128]{2,1,0:T(8,128)S(1)} %copy-done.1, f32[1,128]{1,0:T(1,128)S(1)} %copy-done.4, ...), custom_call_target="tpu_custom_call" | custom-call | flops 2147483648 | bytes 6291456 | tf_op jit(solution)/shard_map/pallas_call | solution.py:514
  94.9 2.1 %last.2.refs_0_ = bf16[256,2048]{1,0:T(8,128)(2,1)} custom-call(s32[1,2]{1,0:T(1,128)S(1)} %copy-done.3, s32[1]{0:T(128)S(6)} %copy.10.dirty, s32[1]{0:T(128)} %bitcast.index_ref, bf16[264,2048]{1,0:T(8,128)(2,1)S(1)} %shard_map.73.own, bf16[264,1280]{1,0:T(8,128)(2,1)S(1)} %collective-permute-done.14.a, bf16[264,1280]{1,0:T(8,128)(2,1)S(1)} %collective-permute-done.15.b), custom_call_target="tpu_custom_call" | custom-call | tf_op jit(solution)/shard_map/last/pallas_call | solution.py:542
  97.0 5.7 %collective-permute-done.7.a = bf16[264,768]{1,0:T(8,128)(2,1)S(1)} collective-permute-done((bf16[264,768]{1,0:T(8,128)(2,1)S(1)}, bf16[264,768]{1,0:T(8,128)(2,1)S(1)}, u32[]{:S(2)}, u32[]{:S(2)}) %collective-permute-start.7) | collective-permute-done | bytes 405536 | tf_op jit(solution)/shard_map/ppermute | solution.py:43
  102.7 1.8 %last.3 = bf16[256,2048]{1,0:T(8,128)(2,1)} custom-call(s32[1,2]{1,0:T(1,128)S(1)} %copy-done.3, s32[1]{0:T(128)S(6)} %copy.10.dirty, s32[1]{0:T(128)} %bitcast.index_ref, bf16[264,2048]{1,0:T(8,128)(2,1)S(1)} %shard_map.73.own, bf16[264,768]{1,0:T(8,128)(2,1)S(1)} %collective-permute-done.7.a, ...), custom_call_target="tpu_custom_call", output_to_operand_aliasing={{}: (6, {})} | custom-call | tf_op jit(solution)/shard_map/last/pallas_call | solution.py:542
  (30 shorter events, 6.8 us)
Async XLA Ops:
  0.0 24.4 %collective-permute-start.1 = (bf16[1024,1024]{1,0:T(8,128)(2,1)}, bf16[1024,1024]{1,0:T(8,128)(2,1)S(1)}, u32[]{:S(2)}, u32[]{:S(2)}) collective-permute-start(bf16[1024,1024]{1,0:T(8,128)(2,1)} %keys.1), channel_id=1, source_target_pairs={{0,1},{1,0},{2,3},{3,2},{4,5},{5,4},{6,7},{7,6},{8,9},{9,8},{10,11... | collective-permute-start | bytes 6291464 | tf_op jit(solution)/shard_map/ppermute | solution.py:43
  0.0 28.1 %collective-permute-start.2 = (bf16[1024,1024]{1,0:T(8,128)(2,1)}, bf16[1024,1024]{1,0:T(8,128)(2,1)}, u32[]{:S(2)}, u32[]{:S(2)}) collective-permute-start(bf16[1024,1024]{1,0:T(8,128)(2,1)} %values.1), channel_id=1, source_target_pairs={{0,1},{1,0},{2,3},{3,2},{4,5},{5,4},{6,7},{7,6},{8,9},{9,8},{10,11... | collective-permute-start | bytes 6291464 | tf_op jit(solution)/shard_map/ppermute | solution.py:43
  1.6 18.5 %collective-permute-start.12 = (bf16[256,1280]{1,0:T(8,128)(2,1)S(1)}, bf16[256,1280]{1,0:T(8,128)(2,1)S(1)}, u32[]{:S(2)}, u32[]{:S(2)}) collective-permute-start(bf16[256,1280]{1,0:T(8,128)(2,1)S(1)} %cut.1), channel_id=1, source_target_pairs={{4,0},{5,1},{6,2},{7,3},{8,4},{9,5},{10,6},{11,7},{12,8},{13,9},{1... | collective-permute-start | bytes 1966088 | tf_op jit(solution)/shard_map/ppermute | solution.py:43
  4.0 3.5 %collective-permute-start = (s32[1,2]{1,0:T(1,128)}, s32[1,2]{1,0:T(1,128)S(1)}, u32[]{:S(2)}, u32[]{:S(2)}) collective-permute-start(s32[1,2]{1,0:T(1,128)} %spans.17), channel_id=1, source_target_pairs={{0,1},{1,0},{2,3},{3,2},{4,5},{5,4},{6,7},{7,6},{8,9},{9,8},{10,11... | collective-permute-start | bytes 32 | tf_op jit(solution)/shard_map/ppermute | solution.py:43
  4.7 25.3 %copy-start.1 = (f32[2,256,128]{2,1,0:T(8,128)S(1)}, f32[2,256,128]{2,1,0:T(8,128)}, u32[]{:S(2)}) copy-start(f32[2,256,128]{2,1,0:T(8,128)} %constant.8.clone.angles.refs_0_.refs_3_) | copy-start | bytes 786436
  7.5 0.7 copy-start.2
  8.2 21.8 %copy-start.3 = (s32[1,2]{1,0:T(1,128)S(1)}, s32[1,2]{1,0:T(1,128)}, u32[]{:S(2)}) copy-start(s32[1,2]{1,0:T(1,128)} %spans.17) | copy-start | bytes 28
  8.2 21.9 %copy-start.4 = (f32[1,128]{1,0:T(1,128)S(1)}, f32[1,128]{1,0:T(1,128)}, u32[]{:S(2)}) copy-start(f32[1,128]{1,0:T(1,128)} %constant.9.clone.freq.refs_1_.refs_4_) | copy-start | bytes 1540
  10.7 38.4 %collective-permute-start.9 = (bf16[328,1024]{1,0:T(8,128)(2,1)S(1)}, bf16[328,1024]{1,0:T(8,128)(2,1)S(1)}, u32[]{:S(2)}, u32[]{:S(2)}) collective-permute-start(bf16[328,1024]{1,0:T(8,128)(2,1)S(1)} %get-tuple-element.16), channel_id=1, source_target_pairs={{1,2},{3,4},{5,6},{7,8},{9,10},{11,12},{13,14},{17,18},{19,20},{21... | collective-permute-start | bytes 2015240 | tf_op jit(solution)/shard_map/ppermute | solution.py:43
  12.0 48.2 %collective-permute-start.11 = (bf16[256,1280]{1,0:T(8,128)(2,1)S(1)}, bf16[256,1280]{1,0:T(8,128)(2,1)}, u32[]{:S(2)}, u32[]{:S(2)}) collective-permute-start(bf16[256,1280]{1,0:T(8,128)(2,1)S(1)} %cut.1), channel_id=1, source_target_pairs={{2,0},{3,1},{6,4},{7,5},{10,8},{11,9},{14,12},{15,13},{18,16},{19,... | collective-permute-start | bytes 1966088 | tf_op jit(solution)/shard_map/ppermute | solution.py:43
  20.1 40.0 %collective-permute-start.13 = (bf16[256,1280]{1,0:T(8,128)(2,1)S(1)}, bf16[256,1280]{1,0:T(8,128)(2,1)}, u32[]{:S(2)}, u32[]{:S(2)}) collective-permute-start(bf16[256,1280]{1,0:T(8,128)(2,1)S(1)} %collective-permute-done.12.refs_8_), channel_id=1, source_target_pairs={{0,2},{1,3},{4,6},{5,7},{8,10},{9,11},{12,14},{13,15},{16,18},{17,... | collective-permute-start | bytes 1966088 | tf_op jit(solution)/shard_map/ppermute | solution.py:43
  24.4 1.3 %copy-start.5 = (bf16[1024,1024]{1,0:T(8,128)(2,1)}, bf16[1024,1024]{1,0:T(8,128)(2,1)S(1)}, u32[]{:S(2)}) copy-start(bf16[1024,1024]{1,0:T(8,128)(2,1)S(1)} %collective-permute-done.1.k_other) | copy-start | bytes 6291460
  25.7 18.8 %collective-permute-start.5 = (bf16[256,768]{1,0:T(8,128)(2,1)}, bf16[256,768]{1,0:T(8,128)(2,1)S(1)}, u32[]{:S(2)}, u32[]{:S(2)}) collective-permute-start(bf16[256,768]{1,0:T(8,128)(2,1)} %get-tuple-element.15), channel_id=1, source_target_pairs={{4,0},{5,1},{6,2},{7,3},{8,4},{9,5},{10,6},{11,7},{12,8},{13,9},{1... | collective-permute-start | bytes 1179656 | tf_op jit(solution)/shard_map/ppermute | solution.py:43
  28.1 9.7 %collective-permute-start.3 = (s32[8]{0:T(128)S(1)}, s32[8]{0:T(128)S(1)}, u32[]{:S(2)}, u32[]{:S(2)}) collective-permute-start(s32[8]{0:T(128)S(1)} %get-tuple-element.14), channel_id=1, source_target_pairs={{2,0},{3,1},{4,2},{5,3},{6,4},{7,5},{8,6},{9,7},{10,8},{11,9},{12,... | collective-permute-start | bytes 104 | tf_op jit(solution)/shard_map/ppermute | solution.py:43
  37.7 5.5 %collective-permute-start.8 = (s32[8]{0:T(128)S(1)}, s32[8]{0:T(128)S(1)}, u32[]{:S(2)}, u32[]{:S(2)}) collective-permute-start(s32[8]{0:T(128)S(1)} %get-tuple-element.14), channel_id=1, source_target_pairs={{4,0},{5,1},{6,2},{7,3},{8,4},{9,5},{10,6},{11,7},{12,8},{13,9},{1... | collective-permute-start | bytes 104 | tf_op jit(solution)/shard_map/ppermute | solution.py:43
  43.2 36.8 %collective-permute-start.4 = (bf16[256,768]{1,0:T(8,128)(2,1)}, bf16[256,768]{1,0:T(8,128)(2,1)S(1)}, u32[]{:S(2)}, u32[]{:S(2)}) collective-permute-start(bf16[256,768]{1,0:T(8,128)(2,1)} %get-tuple-element.15), channel_id=1, source_target_pairs={{2,0},{3,1},{6,4},{7,5},{10,8},{11,9},{14,12},{15,13},{18,16},{19,... | collective-permute-start | bytes 1179656 | tf_op jit(solution)/shard_map/ppermute | solution.py:43
  44.5 35.5 %collective-permute-start.6 = (bf16[256,768]{1,0:T(8,128)(2,1)S(1)}, bf16[256,768]{1,0:T(8,128)(2,1)S(1)}, u32[]{:S(2)}, u32[]{:S(2)}) collective-permute-start(bf16[256,768]{1,0:T(8,128)(2,1)S(1)} %collective-permute-done.5.refs_8_), channel_id=1, source_target_pairs={{0,2},{1,3},{4,6},{5,7},{8,10},{9,11},{12,14},{13,15},{16,18},{17,... | collective-permute-start | bytes 1179656 | tf_op jit(solution)/shard_map/ppermute | solution.py:43
  58.2 36.7 %collective-permute-start.15 = (bf16[264,1280]{1,0:T(8,128)(2,1)S(1)}, bf16[264,1280]{1,0:T(8,128)(2,1)S(1)}, u32[]{:S(2)}, u32[]{:S(2)}) collective-permute-start(bf16[264,1280]{1,0:T(8,128)(2,1)S(1)} %shard_map.77), channel_id=1, source_target_pairs={{0,4},{1,5},{2,6},{3,7},{4,8},{5,9},{6,10},{7,11},{8,12},{9,13},{1... | collective-permute-start | bytes 2027528 | tf_op jit(solution)/shard_map/ppermute | solution.py:43
  61.5 33.4 %collective-permute-start.14 = (bf16[264,1280]{1,0:T(8,128)(2,1)S(1)}, bf16[264,1280]{1,0:T(8,128)(2,1)S(1)}, u32[]{:S(2)}, u32[]{:S(2)}) collective-permute-start(bf16[264,1280]{1,0:T(8,128)(2,1)S(1)} %shard_map.76), channel_id=1, source_target_pairs={{0,2},{1,3},{2,4},{3,5},{4,6},{5,7},{6,8},{7,9},{8,10},{9,11},{10,... | collective-permute-start | bytes 2027528 | tf_op jit(solution)/shard_map/ppermute | solution.py:43
  77.7 10.3 %copy-start = (bf16[256,2048]{1,0:T(8,128)(2,1)S(1)}, bf16[256,2048]{1,0:T(8,128)(2,1)}, u32[]{:S(2)}) copy-start(bf16[256,2048]{1,0:T(8,128)(2,1)} %query.3) | copy-start | bytes 3145732
  77.7 19.3 %collective-permute-start.10 = (bf16[264,768]{1,0:T(8,128)(2,1)S(1)}, bf16[264,768]{1,0:T(8,128)(2,1)S(1)}, u32[]{:S(2)}, u32[]{:S(2)}) collective-permute-start(bf16[264,768]{1,0:T(8,128)(2,1)S(1)} %shard_map.75), channel_id=1, source_target_pairs={{0,4},{1,5},{2,6},{3,7},{4,8},{5,9},{6,10},{7,11},{8,12},{9,13},{1... | collective-permute-start | bytes 1216520 | tf_op jit(solution)/shard_map/ppermute | solution.py:43
  80.6 22.2 %collective-permute-start.7 = (bf16[264,768]{1,0:T(8,128)(2,1)S(1)}, bf16[264,768]{1,0:T(8,128)(2,1)S(1)}, u32[]{:S(2)}, u32[]{:S(2)}) collective-permute-start(bf16[264,768]{1,0:T(8,128)(2,1)S(1)} %shard_map.74), channel_id=1, source_target_pairs={{0,2},{1,3},{2,4},{3,5},{4,6},{5,7},{6,8},{7,9},{8,10},{9,11},{10,... | collective-permute-start | bytes 1216520 | tf_op jit(solution)/shard_map/ppermute | solution.py:43

commit v4 on v3

--- a/solution.py
+++ b/solution.py
@@ -174,16 +174,17 @@
 
     def stage(slot, at):
         some = pl.ds(pl.multiple_of(at * BLOCK_ROWS, BLOCK_ROWS), BLOCK_ROWS)
+        into = slice(slot * BLOCK_ROWS, (slot + 1) * BLOCK_ROWS)
         for i in range(kv_heads):
-            ke[slot, i] = kr[low + i, some, :]
-            ve[slot, i] = vz[low + i, some, :]
-        le[slot] = lv[some, :]
-
-    def masked(slot, keep, fresh):
+            ke[i, into] = kr[low + i, some, :]
+            ve[i, into] = vz[low + i, some, :]
+        le[into] = lv[some, :]
+
+    def masked(keep):
         for i in range(kv_heads):
-            v = jnp.concatenate([ve[slot, i], le[slot]], axis=1)
+            v = jnp.concatenate([ve[i], le[...]], axis=1)
             for g in range(2):
-                add(2 * i + g, ke[slot, i], v, keep, fresh)
+                add(2 * i + g, ke[i], v, keep, True)
 
     def places_at(at):
         pair = [frame.tile(s, at * BLOCK_ROWS) for s in (0, 1)]
@@ -194,7 +195,7 @@
         many(0, 2 * per, True)
     elif kind == "own":
         stage(0, odd * per + block)
-        masked(0, own >= places_at(block), True)
+        masked(own >= places_at(block))
 
         @pl.when(odd == 1)
         def _():
@@ -216,12 +217,13 @@
             live = (row < tail_tile[2]) | (row >= tail_tile[3])
             live = live & (row >= BLOCK_ROWS - reach) & (index > 0)
             c, s = rope_tables(angles, tail_tile[2], wave(list(tail_tile[:2]), freq), 0, 1.0)
-            le[0] = jnp.where(live, 1.0, 0.0).astype(jnp.bfloat16)
+            alive = jnp.where(live, 1.0, 0.0).astype(jnp.bfloat16)
+            le[:BLOCK_ROWS] = alive
             zero = jnp.zeros((BLOCK_ROWS - reach, HEAD_DIMENSION), jnp.bfloat16)
             for i in range(kv_heads):
                 cols = slice((low + i) * HEAD_DIMENSION, (low + i + 1) * HEAD_DIMENSION)
-                ke[0, i] = rotate(jnp.concatenate([zero, tail_k[:, cols]], axis=0), c, s)
-                ve[0, i] = jnp.concatenate([zero, tail_v[:, cols]], axis=0) * le[0]
+                ke[i, :BLOCK_ROWS] = rotate(jnp.concatenate([zero, tail_k[:, cols]], axis=0), c, s)
+                ve[i, :BLOCK_ROWS] = jnp.concatenate([zero, tail_v[:, cols]], axis=0) * alive
 
         stage(1, first)
         inside = block > 0
@@ -231,8 +233,7 @@
         other = [jnp.where(inside, a, b) for a, b in zip(frame.tile(1, row), last)]
         tile = [jnp.where(odd == 1, b, a) for a, b in zip(even, other)]
         before = places(tile, 1, (1, BLOCK_ROWS))
-        masked(0, own - before < WINDOW, True)
-        masked(1, own - places_at(block) < WINDOW, False)
+        masked(own - jnp.concatenate([before, places_at(block)], axis=1) < WINDOW)
 
         @pl.when(odd == 0)
         def _():
@@ -386,7 +387,8 @@
 def last_kernel(rows, low, spans, dirty, index_ref, own, a, b, *refs):
     out, result, sem = refs[-3:]
     index = index_ref[0]
-    heads = result.shape[1] // HEAD_DIMENSION
+    heads = result.shape[0]
+    copies = []
     block = dirty[0]
     first = index * rows + jnp.maximum(block, 0) * BLOCK_ROWS
     row = lax.broadcasted_iota(jnp.int32, (BLOCK_ROWS, LANES), 0) + first
@@ -412,12 +414,11 @@
             + a[:BLOCK_ROWS, cols].astype(jnp.float32)
             + b[:BLOCK_ROWS, cols].astype(jnp.float32)
         )
-        result[:, cols] = jnp.where(keep, number / total, 0.0).astype(result.dtype)
-    copy = pltpu.make_async_copy(
-        result, out.at[:, low * HEAD_DIMENSION : (low + heads) * HEAD_DIMENSION], sem
-    )
-    copy.start()
-    copy.wait()
+        result[head] = jnp.where(keep, number / total, 0.0).astype(result.dtype)
+        copies.append(pltpu.make_async_copy(result.at[head], out.at[:, from_own], sem.at[head]))
+        copies[-1].start()
+    for copy in copies:
+        copy.wait()
 
 
 SMEM = pl.BlockSpec(memory_space=pltpu.SMEM)
@@ -519,9 +520,9 @@
             scratch_shapes=[
                 pltpu.VMEM((2 * heads, BLOCK_ROWS, HEAD_DIMENSION), jnp.bfloat16),
                 pltpu.VMEM((2 * heads, BLOCK_ROWS, HEAD_DIMENSION + LANES), jnp.float32),
-                pltpu.VMEM((edges, heads, BLOCK_ROWS, HEAD_DIMENSION), jnp.bfloat16),
-                pltpu.VMEM((edges, heads, BLOCK_ROWS, HEAD_DIMENSION), jnp.bfloat16),
-                pltpu.VMEM((edges, BLOCK_ROWS, LANES), jnp.bfloat16),
+                pltpu.VMEM((heads, edges * BLOCK_ROWS, HEAD_DIMENSION), jnp.bfloat16),
+                pltpu.VMEM((heads, edges * BLOCK_ROWS, HEAD_DIMENSION), jnp.bfloat16),
+                pltpu.VMEM((edges * BLOCK_ROWS, LANES), jnp.bfloat16),
             ],
             compiler_params=params,
             cost_estimate=pl.CostEstimate(
@@ -545,8 +546,8 @@
                 in_specs=[SMEM] * 3 + [VMEM] * 3 + [HBM] * len(result),
                 out_specs=HBM,
                 scratch_shapes=[
-                    pltpu.VMEM((BLOCK_ROWS, 2 * heads * HEAD_DIMENSION), queries.dtype),
-                    pltpu.SemaphoreType.DMA(()),
+                    pltpu.VMEM((2 * heads, BLOCK_ROWS, HEAD_DIMENSION), queries.dtype),
+                    pltpu.SemaphoreType.DMA((2 * heads,)),
                 ],
                 input_output_aliases={6: 0} if result else {},
                 compiler_params=params,

time: 105 us -> 105 us (level)
  no operation moved by 1% of the time
where the time goes in v4:
time: 105 us
  starting transfers between devices  43.8 us (42%)
  Pallas kernels  36.4 us (35%)
  waiting for transfers between devices  21.3 us (20%)
  local copies, waits for them, and re-layouts  1.97 us (2%)
  between operations  1.12 us (1%)
    ppermute x16, starting transfers between devices, send(): return lax.ppermute(array, 'seq', pairs)  43.8 us
    pallas_call x5, Pallas kernels, visitor(): pl.pallas_call(functools.partial(visit_kernel, kind, step, shards, rows,...  24.1 us
    ppermute x16, waiting for transfers between devices, send(): return lax.ppermute(array, 'seq', pairs)  21.3 us
    pallas_call x1, Pallas kernels, work(): pl.pallas_call(prepare_kernel, out_shape=(by_head, by_head, pltpu.VMEM((2...  4.95 us
    pallas_call x2, Pallas kernels, work(): pl.pallas_call(functools.partial(last_kernel, rows, 2 * low), out_shape=j...  3.66 us
    pallas_call x1, Pallas kernels, work(): pl.pallas_call(pack_kernel, out_shape=[jax.ShapeDtypeStruct((BLOCK_ROWS,...  2.51 us
  transfers between devices with their start and end apart: 16, of which 5 were waited for; matrix products, arithmetic and copies ran while one was open for 0% of the time, Pallas kernels for 33%

profile of v4, /device:TPU:16, one launch (start us, length us, event | category | flops | bytes accessed | tf_op | source)
XLA Modules:
  0.0 104.6 jit_solution(7754252181833614937)
XLA Ops:
  1.6 2.4 %collective-permute-start.12 = (bf16[256,1280]{1,0:T(8,128)(2,1)S(1)}, bf16[256,1280]{1,0:T(8,128)(2,1)S(1)}, u32[]{:S(2)}, u32[]{:S(2)}) collective-permute-start(bf16[256,1280]{1,0:T(8,128)(2,1)S(1)} %cut.1), channel_id=1, source_target_pairs={{4,0},{5,1},{6,2},{7,3},{8,4},{9,5},{10,6},{11,7},{12,8},{13,9},{1... | collective-permute-start | bytes 1966088 | tf_op jit(solution)/shard_map/ppermute | solution.py:43
  4.7 2.8 %collective-permute-done.other = s32[1,2]{1,0:T(1,128)S(1)} collective-permute-done((s32[1,2]{1,0:T(1,128)}, s32[1,2]{1,0:T(1,128)S(1)}, u32[]{:S(2)}, u32[]{:S(2)}) %collective-permute-start) | collective-permute-done | bytes 40 | tf_op jit(solution)/shard_map/ppermute | solution.py:43
  8.2 2.5 %pack.1 = (bf16[256,768]{1,0:T(8,128)(2,1)}, bf16[328,1024]{1,0:T(8,128)(2,1)S(1)}, s32[8]{0:T(128)S(1)}) custom-call(s32[1,2]{1,0:T(1,128)S(1)} %copy-done.2, s32[1,2]{1,0:T(1,128)S(1)} %collective-permute-done.other, s32[1]{0:T(128)S(6)} %copy.10.dirty, bf16[1024,1024]{1,0:T(8,128)(2,1)} %keys.1, bf16[1024,1024]{1,0:T(8,128)(2,1)} %values.1, ...), custom_call_target="tpu_custom_call" | custom-call | flops 1 | bytes 2097152 | tf_op jit(solution)/shard_map/pack/pallas_call | solution.py:462
  13.3 6.9 %collective-permute-done.12.refs_8_ = bf16[256,1280]{1,0:T(8,128)(2,1)S(1)} collective-permute-done((bf16[256,1280]{1,0:T(8,128)(2,1)S(1)}, bf16[256,1280]{1,0:T(8,128)(2,1)S(1)}, u32[]{:S(2)}, u32[]{:S(2)}) %collective-permute-start.12) | collective-permute-done | bytes 655392 | tf_op jit(solution)/shard_map/ppermute | solution.py:43
  20.1 4.2 %collective-permute-start.13 = (bf16[256,1280]{1,0:T(8,128)(2,1)S(1)}, bf16[256,1280]{1,0:T(8,128)(2,1)}, u32[]{:S(2)}, u32[]{:S(2)}) collective-permute-start(bf16[256,1280]{1,0:T(8,128)(2,1)S(1)} %collective-permute-done.12.refs_8_), channel_id=1, source_target_pairs={{0,2},{1,3},{4,6},{5,7},{8,10},{9,11},{12,14},{13,15},{16,18},{17,... | collective-permute-start | bytes 1966088 | tf_op jit(solution)/shard_map/ppermute | solution.py:43
  24.4 1.3 %copy-done.5 = bf16[1024,1024]{1,0:T(8,128)(2,1)} copy-done((bf16[1024,1024]{1,0:T(8,128)(2,1)}, bf16[1024,1024]{1,0:T(8,128)(2,1)S(1)}, u32[]{:S(2)}) %copy-start.5) | copy-done | bytes 2097176
  25.7 2.3 %collective-permute-start.5 = (bf16[256,768]{1,0:T(8,128)(2,1)}, bf16[256,768]{1,0:T(8,128)(2,1)S(1)}, u32[]{:S(2)}, u32[]{:S(2)}) collective-permute-start(bf16[256,768]{1,0:T(8,128)(2,1)} %get-tuple-element.15), channel_id=1, source_target_pairs={{4,0},{5,1},{6,2},{7,3},{8,4},{9,5},{10,6},{11,7},{12,8},{13,9},{1... | collective-permute-start | bytes 1179656 | tf_op jit(solution)/shard_map/ppermute | solution.py:43
  28.1 1.9 %collective-permute-start.3 = (s32[8]{0:T(128)S(1)}, s32[8]{0:T(128)S(1)}, u32[]{:S(2)}, u32[]{:S(2)}) collective-permute-start(s32[8]{0:T(128)S(1)} %get-tuple-element.14), channel_id=1, source_target_pairs={{2,0},{3,1},{4,2},{5,3},{6,4},{7,5},{8,6},{9,7},{10,8},{11,9},{12,... | collective-permute-start | bytes 104 | tf_op jit(solution)/shard_map/ppermute | solution.py:43
  30.0 4.9 %prepare.1 = (bf16[8,2048,128]{2,1,0:T(8,128)(2,1)S(1)}, bf16[8,2048,128]{2,1,0:T(8,128)(2,1)S(1)}, bf16[2048,128]{1,0:T(8,128)(2,1)S(1)}) custom-call(s32[1]{0:T(128)} %bitcast.index_ref, s32[1,2]{1,0:T(1,128)S(1)} %copy-done.3, s32[1,2]{1,0:T(1,128)S(1)} %collective-permute-done.other, f32[2,256,128]{2,1,0:T(8,128)S(1)} %copy-done.1, ...), custom_call_target="tpu_custom_call" | custom-call | flops 16777216 | bytes 20971520 | tf_op jit(solution)/shard_map/prepare/pallas_call | solution.py:494
  35.0 2.7 %collective-permute-done.3.refs_0_ = s32[8]{0:T(128)S(1)} collective-permute-done((s32[8]{0:T(128)S(1)}, s32[8]{0:T(128)S(1)}, u32[]{:S(2)}, u32[]{:S(2)}) %collective-permute-start.3) | collective-permute-done | bytes 64 | tf_op jit(solution)/shard_map/ppermute | solution.py:43
  37.7 2.3 %collective-permute-start.8 = (s32[8]{0:T(128)S(1)}, s32[8]{0:T(128)S(1)}, u32[]{:S(2)}, u32[]{:S(2)}) collective-permute-start(s32[8]{0:T(128)S(1)} %get-tuple-element.14), channel_id=1, source_target_pairs={{4,0},{5,1},{6,2},{7,3},{8,4},{9,5},{10,6},{11,7},{12,8},{13,9},{1... | collective-permute-start | bytes 104 | tf_op jit(solution)/shard_map/ppermute | solution.py:43
  40.1 3.1 %collective-permute-done.8.refs_1_ = s32[8]{0:T(128)S(1)} collective-permute-done((s32[8]{0:T(128)S(1)}, s32[8]{0:T(128)S(1)}, u32[]{:S(2)}, u32[]{:S(2)}) %collective-permute-start.8) | collective-permute-done | bytes 64 | tf_op jit(solution)/shard_map/ppermute | solution.py:43
  44.5 4.6 %collective-permute-start.6 = (bf16[256,768]{1,0:T(8,128)(2,1)S(1)}, bf16[256,768]{1,0:T(8,128)(2,1)S(1)}, u32[]{:S(2)}, u32[]{:S(2)}) collective-permute-start(bf16[256,768]{1,0:T(8,128)(2,1)S(1)} %collective-permute-done.5.refs_8_), channel_id=1, source_target_pairs={{0,2},{1,3},{4,6},{5,7},{8,10},{9,11},{12,14},{13,15},{16,18},{17,... | collective-permute-start | bytes 1179656 | tf_op jit(solution)/shard_map/ppermute | solution.py:43
  49.1 9.1 %shard_map.77 = bf16[264,1280]{1,0:T(8,128)(2,1)S(1)} custom-call(s32[1]{0:T(128)} %bitcast.index_ref, s32[1,2]{1,0:T(1,128)S(1)} %copy-done.3, s32[1,2]{1,0:T(1,128)S(1)} %collective-permute-done.other, s32[1]{0:T(128)S(6)} %copy.10.dirty, s32[8]{0:T(128)S(1)} %collective-permute-done.3.refs_0_, s32[8]{0:T(128)S(1)} %collective-permute-done.8.refs_1_, ...), custom_call_target="tpu_custom_call" | custom-call | flops 1342177280 | bytes 6291456 | tf_op jit(solution)/shard_map/pallas_call | solution.py:515
  58.2 1.9 %collective-permute-start.15 = (bf16[264,1280]{1,0:T(8,128)(2,1)S(1)}, bf16[264,1280]{1,0:T(8,128)(2,1)S(1)}, u32[]{:S(2)}, u32[]{:S(2)}) collective-permute-start(bf16[264,1280]{1,0:T(8,128)(2,1)S(1)} %shard_map.77), channel_id=1, source_target_pairs={{0,4},{1,5},{2,6},{3,7},{4,8},{5,9},{6,10},{7,11},{8,12},{9,13},{1... | collective-permute-start | bytes 2027528 | tf_op jit(solution)/shard_map/ppermute | solution.py:43
  60.2 1.4 %shard_map.76 = bf16[264,1280]{1,0:T(8,128)(2,1)S(1)} custom-call(s32[1]{0:T(128)} %bitcast.index_ref, s32[1,2]{1,0:T(1,128)S(1)} %copy-done.3, s32[1,2]{1,0:T(1,128)S(1)} %collective-permute-done.other, s32[1]{0:T(128)S(6)} %copy.10.dirty, s32[8]{0:T(128)S(1)} %collective-permute-done.3.refs_0_, bf16[256,1280]{1,0:T(8,128)(2,1)} %collective-permute-done.11.refs_1_, ...), custom_call_target="tpu_custom_call" | custom-call | flops 2684354560 | bytes 6291456 | tf_op jit(solution)/shard_map/pallas_call | solution.py:515
  61.6 10.0 %collective-permute-start.14 = (bf16[264,1280]{1,0:T(8,128)(2,1)S(1)}, bf16[264,1280]{1,0:T(8,128)(2,1)S(1)}, u32[]{:S(2)}, u32[]{:S(2)}) collective-permute-start(bf16[264,1280]{1,0:T(8,128)(2,1)S(1)} %shard_map.76), channel_id=1, source_target_pairs={{0,2},{1,3},{2,4},{3,5},{4,6},{5,7},{6,8},{7,9},{8,10},{9,11},{10,... | collective-permute-start | bytes 2027528 | tf_op jit(solution)/shard_map/ppermute | solution.py:43
  71.6 6.1 %shard_map.75 = bf16[264,768]{1,0:T(8,128)(2,1)S(1)} custom-call(s32[1]{0:T(128)} %bitcast.index_ref, s32[1,2]{1,0:T(1,128)S(1)} %copy-done.3, s32[1,2]{1,0:T(1,128)S(1)} %collective-permute-done.other, s32[1]{0:T(128)S(6)} %copy.10.dirty, s32[8]{0:T(128)S(1)} %collective-permute-done.3.refs_0_, s32[8]{0:T(128)S(1)} %collective-permute-done.8.refs_1_, ...), custom_call_target="tpu_custom_call" | custom-call | flops 805306368 | bytes 6291456 | tf_op jit(solution)/shard_map/pallas_call | solution.py:515
  77.7 2.2 %collective-permute-start.10 = (bf16[264,768]{1,0:T(8,128)(2,1)S(1)}, bf16[264,768]{1,0:T(8,128)(2,1)S(1)}, u32[]{:S(2)}, u32[]{:S(2)}) collective-permute-start(bf16[264,768]{1,0:T(8,128)(2,1)S(1)} %shard_map.75), channel_id=1, source_target_pairs={{0,4},{1,5},{2,6},{3,7},{4,8},{5,9},{6,10},{7,11},{8,12},{9,13},{1... | collective-permute-start | bytes 1216520 | tf_op jit(solution)/shard_map/ppermute | solution.py:43
  80.6 7.4 %collective-permute-start.7 = (bf16[264,768]{1,0:T(8,128)(2,1)S(1)}, bf16[264,768]{1,0:T(8,128)(2,1)S(1)}, u32[]{:S(2)}, u32[]{:S(2)}) collective-permute-start(bf16[264,768]{1,0:T(8,128)(2,1)S(1)} %shard_map.74), channel_id=1, source_target_pairs={{0,2},{1,3},{2,4},{3,5},{4,6},{5,7},{6,8},{7,9},{8,10},{9,11},{10,... | collective-permute-start | bytes 1216520 | tf_op jit(solution)/shard_map/ppermute | solution.py:43
  88.0 6.9 %shard_map.73.own = bf16[264,2048]{1,0:T(8,128)(2,1)S(1)} custom-call(s32[1]{0:T(128)} %bitcast.index_ref, s32[1,2]{1,0:T(1,128)S(1)} %copy-done.3, s32[1,2]{1,0:T(1,128)S(1)} %collective-permute-done.other, s32[1]{0:T(128)S(6)} %copy.10.dirty, f32[2,256,128]{2,1,0:T(8,128)S(1)} %copy-done.1, f32[1,128]{1,0:T(1,128)S(1)} %copy-done.4, ...), custom_call_target="tpu_custom_call" | custom-call | flops 2147483648 | bytes 6291456 | tf_op jit(solution)/shard_map/pallas_call | solution.py:515
  94.9 1.9 %last.2.refs_0_ = bf16[256,2048]{1,0:T(8,128)(2,1)} custom-call(s32[1,2]{1,0:T(1,128)S(1)} %copy-done.3, s32[1]{0:T(128)S(6)} %copy.10.dirty, s32[1]{0:T(128)} %bitcast.index_ref, bf16[264,2048]{1,0:T(8,128)(2,1)S(1)} %shard_map.73.own, bf16[264,1280]{1,0:T(8,128)(2,1)S(1)} %collective-permute-done.14.a, bf16[264,1280]{1,0:T(8,128)(2,1)S(1)} %collective-permute-done.15.b), custom_call_target="tpu_custom_call" | custom-call | tf_op jit(solution)/shard_map/last/pallas_call | solution.py:543
  96.9 5.8 %collective-permute-done.7.a = bf16[264,768]{1,0:T(8,128)(2,1)S(1)} collective-permute-done((bf16[264,768]{1,0:T(8,128)(2,1)S(1)}, bf16[264,768]{1,0:T(8,128)(2,1)S(1)}, u32[]{:S(2)}, u32[]{:S(2)}) %collective-permute-start.7) | collective-permute-done | bytes 405536 | tf_op jit(solution)/shard_map/ppermute | solution.py:43
  102.7 1.7 %last.3 = bf16[256,2048]{1,0:T(8,128)(2,1)} custom-call(s32[1,2]{1,0:T(1,128)S(1)} %copy-done.3, s32[1]{0:T(128)S(6)} %copy.10.dirty, s32[1]{0:T(128)} %bitcast.index_ref, bf16[264,2048]{1,0:T(8,128)(2,1)S(1)} %shard_map.73.own, bf16[264,768]{1,0:T(8,128)(2,1)S(1)} %collective-permute-done.7.a, ...), custom_call_target="tpu_custom_call", output_to_operand_aliasing={{}: (6, {})} | custom-call | tf_op jit(solution)/shard_map/last/pallas_call | solution.py:543
  (30 shorter events, 6.8 us)
Async XLA Ops:
  0.0 24.4 %collective-permute-start.1 = (bf16[1024,1024]{1,0:T(8,128)(2,1)}, bf16[1024,1024]{1,0:T(8,128)(2,1)S(1)}, u32[]{:S(2)}, u32[]{:S(2)}) collective-permute-start(bf16[1024,1024]{1,0:T(8,128)(2,1)} %keys.1), channel_id=1, source_target_pairs={{0,1},{1,0},{2,3},{3,2},{4,5},{5,4},{6,7},{7,6},{8,9},{9,8},{10,11... | collective-permute-start | bytes 6291464 | tf_op jit(solution)/shard_map/ppermute | solution.py:43
  0.0 28.1 %collective-permute-start.2 = (bf16[1024,1024]{1,0:T(8,128)(2,1)}, bf16[1024,1024]{1,0:T(8,128)(2,1)}, u32[]{:S(2)}, u32[]{:S(2)}) collective-permute-start(bf16[1024,1024]{1,0:T(8,128)(2,1)} %values.1), channel_id=1, source_target_pairs={{0,1},{1,0},{2,3},{3,2},{4,5},{5,4},{6,7},{7,6},{8,9},{9,8},{10,11... | collective-permute-start | bytes 6291464 | tf_op jit(solution)/shard_map/ppermute | solution.py:43
  1.6 18.5 %collective-permute-start.12 = (bf16[256,1280]{1,0:T(8,128)(2,1)S(1)}, bf16[256,1280]{1,0:T(8,128)(2,1)S(1)}, u32[]{:S(2)}, u32[]{:S(2)}) collective-permute-start(bf16[256,1280]{1,0:T(8,128)(2,1)S(1)} %cut.1), channel_id=1, source_target_pairs={{4,0},{5,1},{6,2},{7,3},{8,4},{9,5},{10,6},{11,7},{12,8},{13,9},{1... | collective-permute-start | bytes 1966088 | tf_op jit(solution)/shard_map/ppermute | solution.py:43
  4.0 3.5 %collective-permute-start = (s32[1,2]{1,0:T(1,128)}, s32[1,2]{1,0:T(1,128)S(1)}, u32[]{:S(2)}, u32[]{:S(2)}) collective-permute-start(s32[1,2]{1,0:T(1,128)} %spans.17), channel_id=1, source_target_pairs={{0,1},{1,0},{2,3},{3,2},{4,5},{5,4},{6,7},{7,6},{8,9},{9,8},{10,11... | collective-permute-start | bytes 32 | tf_op jit(solution)/shard_map/ppermute | solution.py:43
  4.7 25.3 %copy-start.1 = (f32[2,256,128]{2,1,0:T(8,128)S(1)}, f32[2,256,128]{2,1,0:T(8,128)}, u32[]{:S(2)}) copy-start(f32[2,256,128]{2,1,0:T(8,128)} %constant.8.clone.angles.refs_0_.refs_3_) | copy-start | bytes 786436
  7.5 0.7 copy-start.2
  8.2 21.8 %copy-start.3 = (s32[1,2]{1,0:T(1,128)S(1)}, s32[1,2]{1,0:T(1,128)}, u32[]{:S(2)}) copy-start(s32[1,2]{1,0:T(1,128)} %spans.17) | copy-start | bytes 28
  8.2 21.9 %copy-start.4 = (f32[1,128]{1,0:T(1,128)S(1)}, f32[1,128]{1,0:T(1,128)}, u32[]{:S(2)}) copy-start(f32[1,128]{1,0:T(1,128)} %constant.9.clone.freq.refs_1_.refs_4_) | copy-start | bytes 1540
  10.7 38.4 %collective-permute-start.9 = (bf16[328,1024]{1,0:T(8,128)(2,1)S(1)}, bf16[328,1024]{1,0:T(8,128)(2,1)S(1)}, u32[]{:S(2)}, u32[]{:S(2)}) collective-permute-start(bf16[328,1024]{1,0:T(8,128)(2,1)S(1)} %get-tuple-element.16), channel_id=1, source_target_pairs={{1,2},{3,4},{5,6},{7,8},{9,10},{11,12},{13,14},{17,18},{19,20},{21... | collective-permute-start | bytes 2015240 | tf_op jit(solution)/shard_map/ppermute | solution.py:43
  12.0 48.2 %collective-permute-start.11 = (bf16[256,1280]{1,0:T(8,128)(2,1)S(1)}, bf16[256,1280]{1,0:T(8,128)(2,1)}, u32[]{:S(2)}, u32[]{:S(2)}) collective-permute-start(bf16[256,1280]{1,0:T(8,128)(2,1)S(1)} %cut.1), channel_id=1, source_target_pairs={{2,0},{3,1},{6,4},{7,5},{10,8},{11,9},{14,12},{15,13},{18,16},{19,... | collective-permute-start | bytes 1966088 | tf_op jit(solution)/shard_map/ppermute | solution.py:43
  20.1 40.0 %collective-permute-start.13 = (bf16[256,1280]{1,0:T(8,128)(2,1)S(1)}, bf16[256,1280]{1,0:T(8,128)(2,1)}, u32[]{:S(2)}, u32[]{:S(2)}) collective-permute-start(bf16[256,1280]{1,0:T(8,128)(2,1)S(1)} %collective-permute-done.12.refs_8_), channel_id=1, source_target_pairs={{0,2},{1,3},{4,6},{5,7},{8,10},{9,11},{12,14},{13,15},{16,18},{17,... | collective-permute-start | bytes 1966088 | tf_op jit(solution)/shard_map/ppermute | solution.py:43
  24.4 1.3 %copy-start.5 = (bf16[1024,1024]{1,0:T(8,128)(2,1)}, bf16[1024,1024]{1,0:T(8,128)(2,1)S(1)}, u32[]{:S(2)}) copy-start(bf16[1024,1024]{1,0:T(8,128)(2,1)S(1)} %collective-permute-done.1.k_other) | copy-start | bytes 6291460
  25.7 18.8 %collective-permute-start.5 = (bf16[256,768]{1,0:T(8,128)(2,1)}, bf16[256,768]{1,0:T(8,128)(2,1)S(1)}, u32[]{:S(2)}, u32[]{:S(2)}) collective-permute-start(bf16[256,768]{1,0:T(8,128)(2,1)} %get-tuple-element.15), channel_id=1, source_target_pairs={{4,0},{5,1},{6,2},{7,3},{8,4},{9,5},{10,6},{11,7},{12,8},{13,9},{1... | collective-permute-start | bytes 1179656 | tf_op jit(solution)/shard_map/ppermute | solution.py:43
  28.1 9.7 %collective-permute-start.3 = (s32[8]{0:T(128)S(1)}, s32[8]{0:T(128)S(1)}, u32[]{:S(2)}, u32[]{:S(2)}) collective-permute-start(s32[8]{0:T(128)S(1)} %get-tuple-element.14), channel_id=1, source_target_pairs={{2,0},{3,1},{4,2},{5,3},{6,4},{7,5},{8,6},{9,7},{10,8},{11,9},{12,... | collective-permute-start | bytes 104 | tf_op jit(solution)/shard_map/ppermute | solution.py:43
  37.7 5.5 %collective-permute-start.8 = (s32[8]{0:T(128)S(1)}, s32[8]{0:T(128)S(1)}, u32[]{:S(2)}, u32[]{:S(2)}) collective-permute-start(s32[8]{0:T(128)S(1)} %get-tuple-element.14), channel_id=1, source_target_pairs={{4,0},{5,1},{6,2},{7,3},{8,4},{9,5},{10,6},{11,7},{12,8},{13,9},{1... | collective-permute-start | bytes 104 | tf_op jit(solution)/shard_map/ppermute | solution.py:43
  43.2 36.8 %collective-permute-start.4 = (bf16[256,768]{1,0:T(8,128)(2,1)}, bf16[256,768]{1,0:T(8,128)(2,1)S(1)}, u32[]{:S(2)}, u32[]{:S(2)}) collective-permute-start(bf16[256,768]{1,0:T(8,128)(2,1)} %get-tuple-element.15), channel_id=1, source_target_pairs={{2,0},{3,1},{6,4},{7,5},{10,8},{11,9},{14,12},{15,13},{18,16},{19,... | collective-permute-start | bytes 1179656 | tf_op jit(solution)/shard_map/ppermute | solution.py:43
  44.5 35.5 %collective-permute-start.6 = (bf16[256,768]{1,0:T(8,128)(2,1)S(1)}, bf16[256,768]{1,0:T(8,128)(2,1)S(1)}, u32[]{:S(2)}, u32[]{:S(2)}) collective-permute-start(bf16[256,768]{1,0:T(8,128)(2,1)S(1)} %collective-permute-done.5.refs_8_), channel_id=1, source_target_pairs={{0,2},{1,3},{4,6},{5,7},{8,10},{9,11},{12,14},{13,15},{16,18},{17,... | collective-permute-start | bytes 1179656 | tf_op jit(solution)/shard_map/ppermute | solution.py:43
  58.2 36.7 %collective-permute-start.15 = (bf16[264,1280]{1,0:T(8,128)(2,1)S(1)}, bf16[264,1280]{1,0:T(8,128)(2,1)S(1)}, u32[]{:S(2)}, u32[]{:S(2)}) collective-permute-start(bf16[264,1280]{1,0:T(8,128)(2,1)S(1)} %shard_map.77), channel_id=1, source_target_pairs={{0,4},{1,5},{2,6},{3,7},{4,8},{5,9},{6,10},{7,11},{8,12},{9,13},{1... | collective-permute-start | bytes 2027528 | tf_op jit(solution)/shard_map/ppermute | solution.py:43
  61.6 33.4 %collective-permute-start.14 = (bf16[264,1280]{1,0:T(8,128)(2,1)S(1)}, bf16[264,1280]{1,0:T(8,128)(2,1)S(1)}, u32[]{:S(2)}, u32[]{:S(2)}) collective-permute-start(bf16[264,1280]{1,0:T(8,128)(2,1)S(1)} %shard_map.76), channel_id=1, source_target_pairs={{0,2},{1,3},{2,4},{3,5},{4,6},{5,7},{6,8},{7,9},{8,10},{9,11},{10,... | collective-permute-start | bytes 2027528 | tf_op jit(solution)/shard_map/ppermute | solution.py:43
  77.7 10.3 %copy-start = (bf16[256,2048]{1,0:T(8,128)(2,1)S(1)}, bf16[256,2048]{1,0:T(8,128)(2,1)}, u32[]{:S(2)}) copy-start(bf16[256,2048]{1,0:T(8,128)(2,1)} %query.3) | copy-start | bytes 3145732
  77.7 19.2 %collective-permute-start.10 = (bf16[264,768]{1,0:T(8,128)(2,1)S(1)}, bf16[264,768]{1,0:T(8,128)(2,1)S(1)}, u32[]{:S(2)}, u32[]{:S(2)}) collective-permute-start(bf16[264,768]{1,0:T(8,128)(2,1)S(1)} %shard_map.75), channel_id=1, source_target_pairs={{0,4},{1,5},{2,6},{3,7},{4,8},{5,9},{6,10},{7,11},{8,12},{9,13},{1... | collective-permute-start | bytes 1216520 | tf_op jit(solution)/shard_map/ppermute | solution.py:43
  80.6 22.2 %collective-permute-start.7 = (bf16[264,768]{1,0:T(8,128)(2,1)S(1)}, bf16[264,768]{1,0:T(8,128)(2,1)S(1)}, u32[]{:S(2)}, u32[]{:S(2)}) collective-permute-start(bf16[264,768]{1,0:T(8,128)(2,1)S(1)} %shard_map.74), channel_id=1, source_target_pairs={{0,2},{1,3},{2,4},{3,5},{4,6},{5,7},{6,8},{7,9},{8,10},{9,11},{10,... | collective-permute-start | bytes 1216520 | tf_op jit(solution)/shard_map/ppermute | solution.py:43
